TPU v7x, 128 devices: a whole 4x4x4 slice. The times are simulated.
128 devices in a mesh: table: 16 (over y, z), seq: 8 (over x, core).
Axes of the slice: x: 4, y: 4, z: 4, core: 2. Of those that a mesh axis runs over, the one named last changes fastest.
Arguments:
- embed_table: bfloat16 [131072, 512], P('table')
- lookup_ids: int32 [16, 8, 16, 192], P('table', 'seq'), may hold values from 0 to 8191
- counts: int32 [16, 8, 16], P('table', 'seq'), may hold values from 0 to 192, as said below
- event_order: int32 [16, 8, 2048], P('table', 'seq'), may hold values from 0 to 2047, each once within a row
- hist_len: int32 [16], P('table'), may hold values from 4096 to 16384, as said below
- w_uvqk: bfloat16 [512, 2048], replicated, may hold values from -0.25 to 0.25
- w_out: bfloat16 [512, 512], replicated, may hold values from -0.25 to 0.25
Outputs:
- layer_out: bfloat16 [16, 16384, 512], P('table', 'seq')
Inputs may be any that keep to these rules, and one draw needn't show every extreme that they name: For every user and piece the 16 counts sum to 2048; for every piece index one shard gets exactly 192 from every user. Only the first counts[u, p, j] slots of lookup_ids[u, p, j] are read. `hist_len`: some user has exactly 16384 events.
All inputs are finite; a program needn't handle non-finite values.
Results may differ from a plain program's by a relative error of at most 0.0039.
Values may be sent and summed in bfloat16 or wider, within the bound.
No kernel may reach another device: no remote copies, remote signals or barrier semaphores. Data moves between devices by JAX's collectives and lax.ppermute only.
A program may use at most 128 MiB of HBM per device.

v0:
```python
import jax
import jax.numpy as jnp
from jax import lax
from jax.sharding import PartitionSpec as P

HEADS = 4
WINDOW = 1024


def passed_along(value, axis, steps):
    count = lax.axis_size(axis)
    initial, last = (max(0, -steps), min(count, count - steps))
    return lax.ppermute(value, axis, [(source, source + steps) for source in range(initial, last)])


def normalize(values):
    average = jnp.mean(values, axis=-1, keepdims=True)
    centered = values - average
    spread = jnp.mean(centered * centered, axis=-1, keepdims=True)
    return centered * lax.rsqrt(spread + 1e-05)


def attend_block(queries, keyvals, head_count):
    query_rows, width = queries.shape
    key_rows = keyvals.shape[0]
    head_width = width // head_count
    query_heads = queries.reshape(query_rows, head_count, head_width)
    key_heads = keyvals[:, :width].reshape(key_rows, head_count, head_width)
    value_heads = keyvals[:, width:].reshape(key_rows, head_count, head_width)
    scores = jnp.einsum("qhd,khd->hqk", query_heads, key_heads, preferred_element_type=jnp.float32)
    scores = scores * head_width ** (-0.5)
    distance = (
        jnp.arange(query_rows)[:, None] + (key_rows - query_rows) - jnp.arange(key_rows)[None, :]
    )
    inside = (distance >= 0) & (distance < key_rows - query_rows)
    weights = jnp.where(inside[None], jax.nn.silu(scores), 0.0).astype(jnp.bfloat16)
    attended = jnp.einsum("hqk,khd->qhd", weights, value_heads, preferred_element_type=jnp.float32)
    return attended.reshape(query_rows, width)


def local(embed_table, lookup_ids, counts, event_order, hist_len, w_uvqk, w_out):
    shards = lax.axis_size("table")
    capacity = lookup_ids.shape[3]
    tokens = event_order.shape[2]
    width = embed_table.shape[1]
    requests = lookup_ids[0, 0]
    fetched = lax.all_to_all(
        embed_table[lax.all_to_all(requests, "table", split_axis=0, concat_axis=0, tiled=True)],
        "table",
        split_axis=0,
        concat_axis=0,
        tiled=True,
    )
    live_counts = counts[0, 0]
    totals = jnp.cumsum(live_counts)
    starts = totals - live_counts
    event_rank = event_order[0, 0]
    owner_shard = jnp.sum((event_rank[:, None] >= totals[None, :]).astype(jnp.int32), axis=1)
    chosen = owner_shard[:, None] == jnp.arange(shards, dtype=jnp.int32)[None, :]
    slot_start = jnp.sum(jnp.where(chosen, starts[None, :], 0), axis=1)
    slot_index = owner_shard * capacity + event_rank - slot_start
    events = fetched.reshape(shards * capacity, width)[slot_index]
    normed = normalize(events.astype(jnp.float32)).astype(jnp.bfloat16)
    activated = jax.nn.silu(jnp.dot(normed, w_uvqk, preferred_element_type=jnp.float32)).astype(
        jnp.bfloat16
    )
    gate_part = activated[:, :width]
    queries = activated[:, width : 2 * width]
    keyvals = activated[:, 2 * width :]
    before = passed_along(keyvals[tokens - WINDOW :], "seq", 1)
    context = jnp.concatenate([before, keyvals], axis=0)
    blocks = []
    for block_index in range(tokens // WINDOW):
        first = block_index * WINDOW
        blocks.append(
            attend_block(
                queries[first : first + WINDOW], context[first : first + 2 * WINDOW], HEADS
            )
        )
    attended = jnp.concatenate(blocks, axis=0)
    gated_rows = (normalize(attended) * gate_part.astype(jnp.float32)).astype(jnp.bfloat16)
    result = jnp.dot(gated_rows, w_out, preferred_element_type=jnp.float32) + events.astype(
        jnp.float32
    )
    position = lax.axis_index("seq") * tokens + jnp.arange(tokens, dtype=jnp.int32)
    result = jnp.where((position < hist_len[0])[:, None], result, 0.0)
    return result.astype(jnp.bfloat16)[None]


def solution(mesh):
    in_specs = (
        P("table", None),
        P("table", "seq", None, None),
        P("table", "seq", None),
        P("table", "seq", None),
        P("table"),
        P(),
        P(),
    )
    out_specs = P("table", "seq", None)
    return jax.shard_map(local, mesh=mesh, in_specs=in_specs, out_specs=out_specs, check_vma=False)
```

profile of v0, /device:TPU:1, one launch (start us, length us, event | category | flops | bytes accessed | tf_op | source)
XLA Modules:
  0.0 171.6 jit_solution(11083543648184990159)
XLA Ops:
  0.0 0.9 all_to_all.11
  0.9 14.8 %all_to_all.17 = s32[16,1,192]{2,1,0:T(1,128)S(1)} all-to-all(s32[16,1,192]{2,1,0:T(1,128)S(1)} %all_to_all.11), channel_id=1, replica_groups=mesh['table'=16,'seq'=8] {'table'}, dimensions={0} | all-to-all | bytes 24576 | tf_op jit(solution)/shard_map/all_to_all | solution.py:48
  15.7 0.1 fusion.22
  15.8 0.1 reshape.192
  15.9 17.8 %gather_fusion = bf16[3072,512]{1,0:T(8,128)(2,1)} fusion(bf16[8192,512]{1,0:T(8,128)(2,1)} %param.7, s32[3072]{0:T(1024)S(1)} %broadcast_clamp_fusion), kind=kCustom, calls=%fused_computation | custom fusion | bytes 6303744 | tf_op jit(solution)/shard_map/gather | solution.py:48
  33.6 4.6 %all-to-all-start.1 = ((bf16[16,192,512]{2,1,0:T(8,128)(2,1)}), bf16[16,192,512]{2,1,0:T(8,128)(2,1)}, u32[]{:S(2)}, u32[]{:S(2)}) async-start(bf16[16,192,512]{2,1,0:T(8,128)(2,1)} %bitcast.43), calls=%async_computation.1 | async-start | bytes 6291456 | tf_op jit(solution)/shard_map/all_to_all | solution.py:47
  38.3 0.1 copy.23
  38.4 0.1 reduce.1
  39.2 0.6 add_compare_fusion
  39.8 0.1 convert_reduce_fusion.1
  39.9 0.1 select_reduce_fusion
  40.0 3.7 %fusion.2 = pred[1024,2048]{1,0:T(8,128)(4,1)} fusion(s32[1024]{0:T(1024)S(1)} %iota_add_fusion), kind=kLoop, calls=%fused_computation.8 | loop fusion | flops 8388608 | bytes 2101248 | tf_op jit(solution)/shard_map/and | solution.py:35
  43.7 31.7 %all-to-all-done.1 = bf16[16,192,512]{2,1,0:T(8,128)(2,1)} async-done(((bf16[16,192,512]{2,1,0:T(8,128)(2,1)}), bf16[16,192,512]{2,1,0:T(8,128)(2,1)}, u32[]{:S(2)}, u32[]{:S(2)}) %all-to-all-start.1) | async-done | bytes 3145760 | tf_op jit(solution)/shard_map/all_to_all | solution.py:47
  75.5 11.6 %gather_fusion.1 = bf16[2048,512]{1,0:T(8,128)(2,1)} fusion(bf16[3072,512]{1,0:T(8,128)(2,1)} %bitcast.3, s32[2048]{0:T(1024)S(1)} %broadcast_clamp_fusion.1), kind=kCustom, calls=%fused_computation.1 | custom fusion | bytes 4202496 | tf_op jit(solution)/shard_map/gather | solution.py:62
  87.0 2.1 %convert_reduce_fusion = f32[2048]{0:T(1024)S(1)} fusion(bf16[2048,512]{1,0:T(8,128)(2,1)} %gather_fusion.1), kind=kLoop, calls=%fused_computation.11 | loop fusion | flops 2095104 | bytes 2105344 | tf_op jit(solution)/shard_map/reduce_sum | solution.py:17
  89.1 2.5 %fusion.7 = f32[2048]{0:T(1024)S(1)} fusion(bf16[2048,512]{1,0:T(8,128)(2,1)} %gather_fusion.1, f32[2048]{0:T(1024)S(1)} %broadcast_multiply_fusion.1), kind=kLoop, calls=%fused_computation.16 | loop fusion | flops 4192256 | bytes 2113536 | tf_op jit(solution)/shard_map/reduce_sum | solution.py:19
  91.6 8.8 %multiply_convert_fusion = bf16[2048,2048]{0,1:T(8,128)(2,1)S(1)} fusion(bf16[512,2048]{1,0:T(8,128)(2,1)S(1)} %copy-done, bf16[2048,512]{1,0:T(8,128)(2,1)S(1)} %copy-done.1, f32[2048]{0:T(1024)S(1)} %add_rsqrt_fusion.1, f32[2048]{0:T(1024)S(1)} %broadcast_multiply_fusion.1), kind=kOutput, calls=%fused_computation.4 | convolution fusion | flops 4320133120 | bytes 12599296 | tf_op jit(solution)/shard_map/dot_general | solution.py:64
  100.5 1.8 %slice.49 = bf16[1024,1024]{0,1:T(8,128)(2,1)} slice(bf16[2048,2048]{0,1:T(8,128)(2,1)S(1)} %multiply_convert_fusion), slice={[1024:2048], [1024:2048]} | slice | bytes 4194304 | tf_op jit(solution)/shard_map/slice | solution.py:70
  102.3 1.9 %fusion.31 = (bf16[1024,512]{0,1:T(8,128)(2,1)S(1)}, bf16[1024,512]{0,1:T(8,128)(2,1)}) fusion(bf16[2048,2048]{0,1:T(8,128)(2,1)S(1)} %multiply_convert_fusion), kind=kLoop, calls=%fused_computation.58 | loop fusion | bytes 4194304 | tf_op jit(solution)/shard_map/slice | solution.py:77
  104.1 0.6 copy-done.3
  104.7 2.2 %fusion.32 = (bf16[2048,512]{0,1:T(8,128)(2,1)}, bf16[2048,512]{0,1:T(8,128)(2,1)}) fusion(bf16[2048,2048]{0,1:T(8,128)(2,1)S(1)} %multiply_convert_fusion), kind=kLoop, calls=%fused_computation.59 | loop fusion | bytes 8388608 | tf_op jit(solution)/shard_map/slice | solution.py:28
  106.9 9.6 %collective-permute-start = (bf16[1024,1024]{0,1:T(8,128)(2,1)}, bf16[1024,1024]{0,1:T(8,128)(2,1)}, u32[]{:S(2)}, u32[]{:S(2)}) collective-permute-start(bf16[1024,1024]{0,1:T(8,128)(2,1)} %slice.49), channel_id=1, source_target_pairs={{0,1},{1,2},{2,3},{3,4},{4,5},{5,6},{6,7},{8,9},{9,10},{10,11},{11... | collective-permute-start | bytes 6291464 | tf_op jit(solution)/shard_map/ppermute | solution.py:13
  116.5 19.6 %fusion.4 = f32[4,128,1024]{2,1,0:T(8,128)} fusion(bf16[2048,4,128]{0,2,1:T(8,128)(2,1)} %bitcast.53, bf16[1024,4,128]{0,2,1:T(8,128)(2,1)} %bitcast.55, bf16[2048,4,128]{0,2,1:T(8,128)(2,1)} %bitcast.52, pred[1024,2048]{1,0:T(8,128)(4,1)} %fusion.2), kind=kOutput, calls=%fused_computation.13 | convolution fusion | flops 4353687552 | bytes 9437184 | tf_op jit(solution)/shard_map/hqk,khd->qhd/dot_general | solution.py:37
  136.1 3.5 %collective-permute-done = bf16[1024,1024]{0,1:T(8,128)(2,1)} collective-permute-done((bf16[1024,1024]{0,1:T(8,128)(2,1)}, bf16[1024,1024]{0,1:T(8,128)(2,1)}, u32[]{:S(2)}, u32[]{:S(2)}) %collective-permute-start) | collective-permute-done | bytes 2097184 | tf_op jit(solution)/shard_map/ppermute | solution.py:13
  139.6 4.0 %pad_maximum_fusion.1 = (bf16[2048,512]{0,1:T(8,128)(2,1)}, bf16[2048,512]{0,1:T(8,128)(2,1)}) fusion(bf16[2048,1024]{0,1:T(8,128)(2,1)S(1)} %slice-done, bf16[1024,1024]{0,1:T(8,128)(2,1)} %collective-permute-done), kind=kLoop, calls=%fused_computation.27 | loop fusion | flops 8388608 | bytes 10485760 | tf_op jit(solution)/shard_map/concatenate | solution.py:71
  143.6 19.3 %fusion.3 = f32[4,128,1024]{2,1,0:T(8,128)} fusion(bf16[2048,4,128]{0,2,1:T(8,128)(2,1)} %bitcast.51, bf16[1024,4,128]{0,2,1:T(8,128)(2,1)S(1)} %bitcast.54, bf16[2048,4,128]{0,2,1:T(8,128)(2,1)} %bitcast.50, pred[1024,2048]{1,0:T(8,128)(4,1)} %fusion.2), kind=kOutput, calls=%fused_computation.12 | convolution fusion | flops 4353687552 | bytes 9437184 | tf_op jit(solution)/shard_map/hqk,khd->qhd/dot_general | solution.py:37
  163.0 2.6 %fusion.12 = f32[2048]{0:T(1024)S(1)} fusion(f32[1024,512]{0,1:T(8,128)} %bitcast.44, f32[1024,512]{0,1:T(8,128)} %bitcast.47), kind=kLoop, calls=%fused_computation.24 | loop fusion | flops 2095104 | bytes 4202496 | tf_op jit(solution)/shard_map/reduce_sum | solution.py:17
  165.6 0.2 copy-done.4
  165.8 0.6 copy-done.5
  166.4 0.5 multiply_reduce_fusion
  166.9 0.1 copy-done.2
  167.1 4.5 %fusion.11 = bf16[1,2048,512]{2,1,0:T(8,128)(2,1)} fusion(bf16[2048,512]{1,0:T(8,128)(2,1)S(1)} %copy-done.2, bf16[512,512]{1,0:T(8,128)(2,1)S(1)} %copy-done.9, f32[1024,512]{0,1:T(8,128)S(1)} %bitcast.46, f32[1024,512]{0,1:T(8,128)S(1)} %bitcast.49, bf16[2048,2048]{0,1:T(8,128)(2,1)} %copy-done.3, f32[2048]{0:T(1024)S(1)} %add_rsqrt_fusion, ...), kind=kOutput, calls=%fused_computation.23 | convolution fusion | flops 1084227584 | bytes 11028480 | tf_op jit(solution)/shard_map/dot_general | solution.py:82
  (29 shorter events, 0.2 us)
Async XLA Ops:
  0.0 91.6 %copy-start = (bf16[512,2048]{1,0:T(8,128)(2,1)S(1)}, bf16[512,2048]{1,0:T(8,128)(2,1)}, u32[]{:S(2)}) copy-start(bf16[512,2048]{1,0:T(8,128)(2,1)} %param.12) | copy-start | bytes 6291460
  33.6 4.6 %copy-start.8 = (s32[1,1,16]{2,1,0:T(1,128)S(1)}, s32[1,1,16]{2,1,0:T(1,128)}, u32[]{:S(2)}) copy-start(s32[1,1,16]{2,1,0:T(1,128)} %param.9) | copy-start | bytes 196
  33.6 6.1 %copy-start.6 = (s32[1,1,2048]{2,1,0:T(1,128)S(1)}, s32[1,1,2048]{2,1,0:T(1,128)}, u32[]{:S(2)}) copy-start(s32[1,1,2048]{2,1,0:T(1,128)} %param.10) | copy-start | bytes 24580
  33.6 41.8 %all-to-all-start.1 = ((bf16[16,192,512]{2,1,0:T(8,128)(2,1)}), bf16[16,192,512]{2,1,0:T(8,128)(2,1)}, u32[]{:S(2)}, u32[]{:S(2)}) async-start(bf16[16,192,512]{2,1,0:T(8,128)(2,1)} %bitcast.43), calls=%async_computation.1 | async-start | bytes 6291456 | tf_op jit(solution)/shard_map/all_to_all | solution.py:47
  87.0 4.6 %copy-start.1 = (bf16[2048,512]{1,0:T(8,128)(2,1)S(1)}, bf16[2048,512]{1,0:T(8,128)(2,1)}, u32[]{:S(2)}) copy-start(bf16[2048,512]{1,0:T(8,128)(2,1)} %gather_fusion.1) | copy-start | bytes 6291460
  100.5 4.2 %copy-start.3 = (bf16[2048,2048]{0,1:T(8,128)(2,1)}, bf16[2048,2048]{0,1:T(8,128)(2,1)S(1)}, u32[]{:S(2)}) copy-start(bf16[2048,2048]{0,1:T(8,128)(2,1)S(1)} %multiply_convert_fusion) | copy-start | bytes 25165828
  106.9 32.7 %collective-permute-start = (bf16[1024,1024]{0,1:T(8,128)(2,1)}, bf16[1024,1024]{0,1:T(8,128)(2,1)}, u32[]{:S(2)}, u32[]{:S(2)}) collective-permute-start(bf16[1024,1024]{0,1:T(8,128)(2,1)} %slice.49), channel_id=1, source_target_pairs={{0,1},{1,2},{2,3},{3,4},{4,5},{5,6},{6,7},{8,9},{9,10},{10,11},{11... | collective-permute-start | bytes 6291464 | tf_op jit(solution)/shard_map/ppermute | solution.py:13
  136.1 3.5 %slice-start = ((bf16[2048,2048]{0,1:T(8,128)(2,1)}), bf16[2048,1024]{0,1:T(8,128)(2,1)S(1)}, s32[]{:S(2)}) async-start(bf16[2048,2048]{0,1:T(8,128)(2,1)} %copy-done.3), calls=%async_computation.2 | async-start | bytes 8388608 | tf_op jit(solution)/shard_map/slice | solution.py:69
  162.9 2.9 %copy-start.4 = (f32[4,128,1024]{2,1,0:T(8,128)S(1)}, f32[4,128,1024]{2,1,0:T(8,128)}, u32[]{:S(2)}) copy-start(f32[4,128,1024]{2,1,0:T(8,128)} %fusion.4) | copy-start | bytes 6291460
  162.9 3.5 %copy-start.5 = (f32[4,128,1024]{2,1,0:T(8,128)S(1)}, f32[4,128,1024]{2,1,0:T(8,128)}, u32[]{:S(2)}) copy-start(f32[4,128,1024]{2,1,0:T(8,128)} %fusion.3) | copy-start | bytes 6291460
  162.9 4.1 %copy-start.2 = (bf16[2048,512]{1,0:T(8,128)(2,1)S(1)}, bf16[2048,512]{1,0:T(8,128)(2,1)}, u32[]{:S(2)}) copy-start(bf16[2048,512]{1,0:T(8,128)(2,1)} %gather_fusion.1) | copy-start | bytes 6291460
  162.9 4.1 %copy-start.7 = (pred[2048]{0:T(1024)(128)(4,1)S(1)}, pred[2048]{0:T(1024)(128)(4,1)}, u32[]{:S(2)}) copy-start(pred[2048]{0:T(1024)(128)(4,1)} %add_compare_fusion) | copy-start | bytes 6148
  162.9 4.2 %copy-start.9 = (bf16[512,512]{1,0:T(8,128)(2,1)S(1)}, bf16[512,512]{1,0:T(8,128)(2,1)}, u32[]{:S(2)}) copy-start(bf16[512,512]{1,0:T(8,128)(2,1)} %param.13) | copy-start | bytes 1572868
where the time goes:
time: 172 us
  matrix products  52.2 us (30%)
  local copies, waits for them, and re-layouts  37.8 us (22%)
  waiting for transfers between devices  35.2 us (20%)
  other arithmetic  16.5 us (10%)
  blocking collectives  14.8 us (9%)
  starting transfers between devices  14.2 us (8%)
    dot_general x2, matrix products, attend_block(): jnp.einsum('hqk,khd->qhd', weights, value_heads, preferred_element_type=j...  38.9 us
    all_to_all x1, waiting for transfers between devices, local(): lax.all_to_all(embed_table[lax.all_to_all(requests, 'table', split_axis=0...  31.7 us
    gather x1, local copies, waits for them, and re-layouts, local(): embed_table[lax.all_to_all(requests, 'table', split_axis=0, concat_axis=0...  17.8 us
    all_to_all x1, blocking collectives, local(): lax.all_to_all(requests, 'table', split_axis=0, concat_axis=0, tiled=True)  14.8 us
    gather x1, local copies, waits for them, and re-layouts, local(): events = fetched.reshape(shards * capacity, width)[slot_index]  11.6 us
    ppermute x1, starting transfers between devices, passed_along(): lax.ppermute(value, axis, [(source, source + steps) for source in range(i...  9.58 us
    dot_general x1, matrix products, local(): jnp.dot(normed, w_uvqk, preferred_element_type=jnp.float32)  8.83 us
    reduce_sum x2, other arithmetic, normalize(): average = jnp.mean(values, axis=-1, keepdims=True)  4.69 us
  transfers between devices with their start and end apart: 2, of which 2 were waited for; matrix products, arithmetic and copies ran while one was open for 14% of the time, Pallas kernels for 0%

commit v1 on v0

v1 whole, which is shorter than its diff:
```python
import jax
import jax.numpy as jnp
from jax import lax
from jax.experimental import pallas as pl
from jax.experimental.pallas import tpu as pltpu
from jax.sharding import PartitionSpec as P

HEADS = 4
WINDOW = 1024
TILE = 256
LANES = 128
MIB = 1 << 20
F32 = jnp.float32
BF16 = jnp.bfloat16
VMEM = pl.BlockSpec(memory_space=pltpu.VMEM)
SMEM = pl.BlockSpec(memory_space=pltpu.SMEM)
ANY = pl.BlockSpec(memory_space=pl.ANY)


def passed_along(value, axis, steps):
    count = lax.axis_size(axis)
    initial, last = (max(0, -steps), min(count, count - steps))
    return lax.ppermute(value, axis, [(source, source + steps) for source in range(initial, last)])


def normalize(values):
    average = jnp.mean(values, axis=-1, keepdims=True)
    centered = values - average
    spread = jnp.mean(centered * centered, axis=-1, keepdims=True)
    return centered * lax.rsqrt(spread + 1e-05)


def silu(values, scale=1.0):
    half = values * (0.5 * scale)
    return half + half * jnp.tanh(half)


def dot(a, b):
    return jnp.dot(a, b, preferred_element_type=F32)


def dot_nt(a, b):
    return lax.dot_general(a, b, (((1,), (1,)), ((), ())), preferred_element_type=F32)


def spread_rows(source, target, first, count):
    step = 32
    parts = source.shape[1] // LANES

    @pl.loop(0, count // step)
    def _(i):
        row = pl.multiple_of(first + i * step, step)
        block = source[pl.ds(row, step), :].astype(F32)
        for k in range(parts):
            target[pl.ds(parts * row + k, step, stride=parts), :] = block[
                :, k * LANES : (k + 1) * LANES
            ]


def pick_rows(indices, source, target, count, parts):
    unroll = 32

    @pl.loop(0, count // unroll)
    def _(i):
        for u in range(unroll):
            j = i * unroll + u
            r = indices[j]
            target[pl.ds(pl.multiple_of(parts * j, parts), parts), :] = source[
                pl.ds(pl.multiple_of(parts * r, parts), parts), :
            ]


def join_rows(source, target, first, count, parts):
    step = 32

    @pl.loop(0, count // step)
    def _(i):
        row = pl.multiple_of(i * step, step)
        for k in range(parts):
            target[pl.ds(row, step), k * LANES : (k + 1) * LANES] = source[
                pl.ds(parts * (first + row) + k, step, stride=parts), :
            ].astype(BF16)


def gather_rows(table, ids):
    rows, width = table.shape
    count = ids.shape[0]
    parts = width // LANES
    chunks = 8
    size = rows // chunks

    def kernel(ids_ref, table_ref, out_ref, held, wide, picked, sems):
        copies = [
            pltpu.make_async_copy(
                table_ref.at[pl.ds(c * size, size)], held.at[pl.ds(c * size, size)], sems.at[c]
            )
            for c in range(chunks)
        ]
        for copy in copies:
            copy.start()
        for c in range(chunks):
            copies[c].wait()
            spread_rows(held, wide, c * size, size)
        pick_rows(ids_ref, wide, picked, count, parts)
        join_rows(picked, out_ref, 0, count, parts)

    return pl.pallas_call(
        kernel,
        out_shape=jax.ShapeDtypeStruct((count, width), BF16),
        in_specs=[SMEM, ANY],
        out_specs=VMEM,
        scratch_shapes=[
            pltpu.VMEM((rows, width), BF16),
            pltpu.VMEM((rows * parts, LANES), F32),
            pltpu.VMEM((count * parts, LANES), F32),
            pltpu.SemaphoreType.DMA((chunks,)),
        ],
        compiler_params=pltpu.CompilerParams(vmem_limit_bytes=40 * MIB),
        name="gather_rows",
    )(ids, table)


def order_rows(fetched, slots):
    count, width = fetched.shape
    tokens = slots.shape[0]
    parts = width // LANES
    chunks = 6
    size = count // chunks
    half = tokens // 2

    def kernel(slots_ref, rows_ref, low_ref, high_ref, held, wide, picked, sems):
        copies = [
            pltpu.make_async_copy(
                rows_ref.at[pl.ds(c * size, size)], held.at[pl.ds(c * size, size)], sems.at[c]
            )
            for c in range(chunks)
        ]
        for copy in copies:
            copy.start()
        for c in range(chunks):
            copies[c].wait()
            spread_rows(held, wide, c * size, size)
        pick_rows(slots_ref, wide, picked, tokens, parts)
        join_rows(picked, low_ref, 0, half, parts)
        join_rows(picked, high_ref, half, half, parts)

    out = jax.ShapeDtypeStruct((half, width), BF16)
    return pl.pallas_call(
        kernel,
        out_shape=(out, out),
        in_specs=[SMEM, ANY],
        out_specs=(VMEM, VMEM),
        scratch_shapes=[
            pltpu.VMEM((count, width), BF16),
            pltpu.VMEM((count * parts, LANES), F32),
            pltpu.VMEM((tokens * parts, LANES), F32),
            pltpu.SemaphoreType.DMA((chunks,)),
        ],
        compiler_params=pltpu.CompilerParams(vmem_limit_bytes=32 * MIB),
        name="order_rows",
    )(slots, fetched)


def lower_mask():
    row = lax.broadcasted_iota(jnp.int32, (TILE, TILE), 0)
    column = lax.broadcasted_iota(jnp.int32, (TILE, TILE), 1)
    return column <= row


def finish(attended, gate, events, w_out, limit, first):
    gated = (normalize(attended) * gate.astype(F32)).astype(BF16)
    result = dot(gated, w_out) + events.astype(F32)
    position = first + lax.broadcasted_iota(jnp.int32, result.shape, 0)
    return jnp.where(position < limit, result, 0.0).astype(BF16)


def own_part(limit, low, high, w_uvqk, w_out):
    half, width = low.shape
    tokens = 2 * half
    head = width // HEADS
    scale = head ** (-0.5)
    reach = WINDOW // TILE
    tiles = tokens // TILE

    def kernel(
        limit_ref, low_ref, high_ref, w_ref, wo_ref, out_ref, part_ref, query_ref, gate_ref, act, done, sem
    ):
        for source, first in ((low_ref, 0), (high_ref, half)):

            @pl.loop(0, half // TILE)
            def _(i):
                row = pl.multiple_of(i * TILE, TILE)
                normed = normalize(source[pl.ds(row, TILE), :].astype(F32)).astype(BF16)
                for k in range(4):
                    cols = slice(k * width, (k + 1) * width)
                    act[pl.ds(first + row, TILE), cols] = silu(dot(normed, w_ref[:, cols])).astype(BF16)

        mask = lower_mask()

        def cols_of(k, h):
            return slice(k * width + h * head, k * width + (h + 1) * head)

        for t in range(reach):
            rows = slice(t * TILE, (t + 1) * TILE)
            for h in range(HEADS):
                query = act[rows, cols_of(1, h)]
                scores = dot_nt(query, act[0 : (t + 1) * TILE, cols_of(2, h)])
                weights = silu(scores, scale)
                diagonal = jnp.where(mask, weights[:, t * TILE :], 0.0).astype(BF16)
                total = dot(diagonal, act[rows, cols_of(3, h)])
                if t:
                    total += dot(weights[:, : t * TILE].astype(BF16), act[0 : t * TILE, cols_of(3, h)])
                part_ref[rows, h * head : (h + 1) * head] = total
        query_ref[...] = act[0:half, width : 2 * width]
        gate_ref[...] = act[0:half, 0:width]

        @pl.loop(0, tiles - reach)
        def _(i):
            t = i + reach
            row = pl.multiple_of(t * TILE, TILE)
            back = pl.multiple_of(i * TILE, TILE)
            pieces = []
            for h in range(HEADS):
                query = act[pl.ds(row, TILE), cols_of(1, h)]
                edge = dot_nt(query, act[pl.ds(back, TILE), cols_of(2, h)])
                inner = dot_nt(query, act[pl.ds(back + TILE, WINDOW - TILE), cols_of(2, h)])
                last = dot_nt(query, act[pl.ds(row, TILE), cols_of(2, h)])
                both = silu(jnp.where(mask, last, edge), scale)
                total = dot(
                    silu(inner, scale).astype(BF16),
                    act[pl.ds(back + TILE, WINDOW - TILE), cols_of(3, h)],
                )
                total += dot(
                    jnp.where(mask, both, 0.0).astype(BF16), act[pl.ds(row, TILE), cols_of(3, h)]
                )
                total += dot(
                    jnp.where(mask, 0.0, both).astype(BF16), act[pl.ds(back, TILE), cols_of(3, h)]
                )
                pieces.append(total)
            done[pl.ds(back, TILE), :] = finish(
                jnp.concatenate(pieces, axis=1),
                act[pl.ds(row, TILE), 0:width],
                high_ref[pl.ds(back, TILE), :],
                wo_ref[...],
                limit_ref[0],
                row,
            )

        copy = pltpu.make_async_copy(done, out_ref.at[pl.ds(half, half)], sem)
        copy.start()
        copy.wait()

    return pl.pallas_call(
        kernel,
        out_shape=(
            jax.ShapeDtypeStruct((tokens, width), BF16),
            jax.ShapeDtypeStruct((half, width), F32),
            jax.ShapeDtypeStruct((half, width), BF16),
            jax.ShapeDtypeStruct((half, width), BF16),
        ),
        in_specs=[SMEM, VMEM, VMEM, VMEM, VMEM],
        out_specs=(ANY, VMEM, VMEM, VMEM),
        scratch_shapes=[
            pltpu.VMEM((tokens, 4 * width), BF16),
            pltpu.VMEM((half, width), BF16),
            pltpu.SemaphoreType.DMA,
        ],
        compiler_params=pltpu.CompilerParams(vmem_limit_bytes=36 * MIB),
        cost_estimate=pl.CostEstimate(
            flops=14_000_000_000, bytes_accessed=12_000_000, transcendentals=12_000_000
        ),
        name="own_part",
    )(limit, low, high, w_uvqk, w_out)


def halo_part(limit, before, part, query, gate, low, w_uvqk, w_out, out):
    half, width = low.shape
    head = width // HEADS
    scale = head ** (-0.5)
    reach = WINDOW // TILE

    def kernel(
        limit_ref, before_ref, part_ref, query_ref, gate_ref, low_ref, w_ref, wo_ref, _, out_ref, keyvals, done, sem
    ):
        @pl.loop(0, half // TILE)
        def _(i):
            row = pl.multiple_of(i * TILE, TILE)
            normed = normalize(before_ref[pl.ds(row, TILE), :].astype(F32)).astype(BF16)
            for k in range(2):
                cols = slice((k + 2) * width, (k + 3) * width)
                keyvals[pl.ds(row, TILE), k * width : (k + 1) * width] = silu(
                    dot(normed, w_ref[:, cols])
                ).astype(BF16)

        mask = lower_mask()
        for t in range(reach):
            rows = slice(t * TILE, (t + 1) * TILE)
            pieces = []
            for h in range(HEADS):
                cols = slice(h * head, (h + 1) * head)
                vcols = slice(width + h * head, width + (h + 1) * head)
                weights = silu(dot_nt(query_ref[rows, cols], keyvals[t * TILE :, cols]), scale)
                edge = jnp.where(mask, 0.0, weights[:, :TILE]).astype(BF16)
                total = part_ref[rows, cols] + dot(edge, keyvals[rows, vcols])
                if t + 1 < reach:
                    total += dot(weights[:, TILE:].astype(BF16), keyvals[(t + 1) * TILE :, vcols])
                pieces.append(total)
            done[rows, :] = finish(
                jnp.concatenate(pieces, axis=1),
                gate_ref[rows, :],
                low_ref[rows, :],
                wo_ref[...],
                limit_ref[0],
                t * TILE,
            )
        copy = pltpu.make_async_copy(done, out_ref.at[pl.ds(0, half)], sem)
        copy.start()
        copy.wait()

    return pl.pallas_call(
        kernel,
        out_shape=jax.ShapeDtypeStruct(out.shape, out.dtype),
        in_specs=[SMEM, VMEM, VMEM, VMEM, VMEM, VMEM, VMEM, VMEM, ANY],
        out_specs=ANY,
        scratch_shapes=[
            pltpu.VMEM((half, 2 * width), BF16),
            pltpu.VMEM((half, width), BF16),
            pltpu.SemaphoreType.DMA,
        ],
        input_output_aliases={8: 0},
        compiler_params=pltpu.CompilerParams(vmem_limit_bytes=36 * MIB),
        name="halo_part",
    )(limit, before, part, query, gate, low, w_uvqk, w_out, out)


def local(embed_table, lookup_ids, counts, event_order, hist_len, w_uvqk, w_out):
    shards = lax.axis_size("table")
    capacity = lookup_ids.shape[3]
    tokens = event_order.shape[2]
    width = embed_table.shape[1]
    requests = lax.all_to_all(lookup_ids[0, 0], "table", split_axis=0, concat_axis=0, tiled=True)
    requests = jnp.clip(requests.reshape(shards * capacity), 0, embed_table.shape[0] - 1)
    found = gather_rows(embed_table, requests)
    fetched = lax.all_to_all(
        found.reshape(shards, capacity, width), "table", split_axis=0, concat_axis=0, tiled=True
    )
    live_counts = counts[0, 0]
    totals = jnp.cumsum(live_counts)
    starts = totals - live_counts
    event_rank = event_order[0, 0]
    owner_shard = jnp.sum((event_rank[:, None] >= totals[None, :]).astype(jnp.int32), axis=1)
    chosen = owner_shard[:, None] == jnp.arange(shards, dtype=jnp.int32)[None, :]
    slot_start = jnp.sum(jnp.where(chosen, starts[None, :], 0), axis=1)
    slot_index = owner_shard * capacity + event_rank - slot_start
    low, high = order_rows(fetched.reshape(shards * capacity, width), slot_index)
    before = passed_along(high, "seq", 1)
    limit = hist_len - lax.axis_index("seq") * tokens
    out, part, query, gate = own_part(limit, low, high, w_uvqk, w_out)
    result = halo_part(limit, before, part, query, gate, low, w_uvqk, w_out, out)
    return result[None]


def solution(mesh):
    in_specs = (
        P("table", None),
        P("table", "seq", None, None),
        P("table", "seq", None),
        P("table", "seq", None),
        P("table"),
        P(),
        P(),
    )
    out_specs = P("table", "seq", None)
    return jax.shard_map(local, mesh=mesh, in_specs=in_specs, out_specs=out_specs, check_vma=False)
```

time: 172 us -> 116 us (0.67)
  matrix products: 52.2 us -> 0 us
  Pallas kernels: 0 us -> 44.7 us
  local copies, waits for them, and re-layouts: 37.8 us -> 5.94 us
  other arithmetic: 16.5 us -> 0.42 us
    dot_general x4 -> x0, matrix products: 52.2 us -> none  [the longest x2 38.9 us: attend_block(): jnp.einsum('hqk,khd->qhd', weights, value_heads, preferred_element_type=j...]
    pallas_call x0 -> x4, Pallas kernels: none -> 44.7 us  [the longest x1 22.2 us: own_part(): pl.pallas_call(kernel, out_shape=(jax.ShapeDtypeStruct((tokens, width), B...]
    gather x2 -> x0, local copies, waits for them, and re-layouts: 29.3 us -> none  [the longest x1 17.8 us: local(): embed_table[lax.all_to_all(requests, 'table', split_axis=0, concat_axis=0...]
    reduce_sum x4 -> x0, other arithmetic: 7.69 us -> none  [the longest x2 4.69 us: normalize(): average = jnp.mean(values, axis=-1, keepdims=True)]
    slice x5 -> x0, local copies, waits for them, and re-layouts: 5.87 us -> none  [the longest x1 2.23 us: attend_block(): key_heads = keyvals[:, :width].reshape(key_rows, head_count, head_width)]
    all_to_all x1, waiting for transfers between devices: 31.7 us -> 36 us  [local(): lax.all_to_all(found.reshape(shards, capacity, width), 'table', split_axi...]
    concatenate x1 -> x0, other arithmetic: 4.04 us -> none  [local(): context = jnp.concatenate([before, keyvals], axis=0)]
    and x1 -> x0, other arithmetic: 3.73 us -> none  [attend_block(): inside = (distance >= 0) & (distance < key_rows - query_rows)]
  transfers between devices with their start and end apart: 2 -> 2, of which waited for: 2 -> 1; matrix products, arithmetic and copies ran while one was open for 14% -> 0% of each run, Pallas kernels for 0% -> 19%
where the time goes in v1:
time: 116 us
  Pallas kernels  44.7 us (39%)
  waiting for transfers between devices  36 us (31%)
  blocking collectives  14.8 us (13%)
  starting transfers between devices  13.3 us (11%)
  local copies, waits for them, and re-layouts  5.94 us (5%)
    all_to_all x1, waiting for transfers between devices, local(): lax.all_to_all(found.reshape(shards, capacity, width), 'table', split_axi...  36 us
    pallas_call x1, Pallas kernels, own_part(): pl.pallas_call(kernel, out_shape=(jax.ShapeDtypeStruct((tokens, width), B...  22.2 us
    all_to_all x1, blocking collectives, local(): lax.all_to_all(lookup_ids[0, 0], 'table', split_axis=0, concat_axis=0, ti...  14.8 us
    pallas_call x1, Pallas kernels, halo_part(): pl.pallas_call(kernel, out_shape=jax.ShapeDtypeStruct(out.shape, out.dtyp...  9.44 us
    ppermute x1, starting transfers between devices, passed_along(): lax.ppermute(value, axis, [(source, source + steps) for source in range(i...  9.42 us
    pallas_call x1, Pallas kernels, gather_rows(): pl.pallas_call(kernel, out_shape=jax.ShapeDtypeStruct((count, width), BF1...  8.18 us
    unnamed x12, local copies, waits for them, and re-layouts  5.06 us
    pallas_call x1, Pallas kernels, order_rows(): pl.pallas_call(kernel, out_shape=(out, out), in_specs=[SMEM, ANY], out_sp...  4.85 us
  transfers between devices with their start and end apart: 2, of which 1 were waited for; matrix products, arithmetic and copies ran while one was open for 0% of the time, Pallas kernels for 19%

profile of v1, /device:TPU:1, one launch (start us, length us, event | category | flops | bytes accessed | tf_op | source)
XLA Modules:
  0.0 116.1 jit_solution(16363758624256819912)
XLA Ops:
  0.0 0.7 all_to_all.9
  0.7 14.8 %all_to_all.14 = s32[16,1,192]{2,1,0:T(1,128)S(1)} all-to-all(s32[16,1,192]{2,1,0:T(1,128)S(1)} %all_to_all.9), channel_id=1, replica_groups=mesh['table'=16,'seq'=8] {'table'}, dimensions={0} | all-to-all | bytes 24576 | tf_op jit(solution)/shard_map/all_to_all | solution.py:341
  15.6 0.1 clamp_reduce_fusion
  15.6 0.1 min.12.ids_ref
  15.7 0.0 copy-start.1
  15.7 3.4 %copy-done.1 = bf16[8192,512]{1,0:T(8,128)(2,1)S(1)} copy-done((bf16[8192,512]{1,0:T(8,128)(2,1)S(1)}, bf16[8192,512]{1,0:T(8,128)(2,1)}, u32[]{:S(2)}) %copy-start.1) | copy-done | bytes 8388632
  19.1 8.2 %gather_rows.1 = bf16[3072,512]{1,0:T(8,128)(2,1)S(1)} custom-call(s32[3072]{0:T(1024)S(1)} %min.12.ids_ref, bf16[8192,512]{1,0:T(8,128)(2,1)S(1)} %copy-done.1), custom_call_target="tpu_custom_call" | custom-call | tf_op jit(solution)/shard_map/gather_rows/pallas_call | solution.py:107
  27.3 0.0 copy-start
  27.3 1.7 %copy-done = bf16[3072,512]{1,0:T(8,128)(2,1)} copy-done((bf16[3072,512]{1,0:T(8,128)(2,1)}, bf16[3072,512]{1,0:T(8,128)(2,1)S(1)}, u32[]{:S(2)}) %copy-start) | copy-done | bytes 3145752
  28.9 0.0 copy-start.5
  28.9 0.0 copy-start.4
  28.9 3.9 %all-to-all-start.1 = ((bf16[16,192,512]{2,1,0:T(8,128)(2,1)}), bf16[16,192,512]{2,1,0:T(8,128)(2,1)S(1)}, u32[]{:S(2)}, u32[]{:S(2)}) async-start(bf16[16,192,512]{2,1,0:T(8,128)(2,1)} %bitcast.11), calls=%async_computation.1 | async-start | bytes 6291456 | tf_op jit(solution)/shard_map/all_to_all | solution.py:344
  33.5 0.0 copy-done.5
  33.5 0.1 copy.12
  33.6 0.1 reduce
  33.7 0.0 copy-done.4
  33.7 0.1 convert_reduce_fusion
  33.9 0.1 select_reduce_fusion
  34.0 36.0 %all-to-all-done.1 = bf16[16,192,512]{2,1,0:T(8,128)(2,1)S(1)} async-done(((bf16[16,192,512]{2,1,0:T(8,128)(2,1)}), bf16[16,192,512]{2,1,0:T(8,128)(2,1)S(1)}, u32[]{:S(2)}, u32[]{:S(2)}) %all-to-all-start.1) | async-done | bytes 3145760 | tf_op jit(solution)/shard_map/all_to_all | solution.py:344
  70.0 0.0 copy-start.2
  70.0 0.0 copy-start.3
  70.0 4.8 %order_rows.1 = (bf16[1024,512]{1,0:T(8,128)(2,1)S(1)}, bf16[1024,512]{1,0:T(8,128)(2,1)S(1)}) custom-call(s32[2048]{0:T(1024)S(1)} %add_subtract_fusion.slots_ref, bf16[3072,512]{1,0:T(8,128)(2,1)S(1)} %bitcast.10), custom_call_target="tpu_custom_call" | custom-call | tf_op jit(solution)/shard_map/order_rows/pallas_call | solution.py:148
  74.8 9.4 %collective-permute-start = (bf16[1024,512]{1,0:T(8,128)(2,1)S(1)}, bf16[1024,512]{1,0:T(8,128)(2,1)S(1)}, u32[]{:S(2)}, u32[]{:S(2)}) collective-permute-start(bf16[1024,512]{1,0:T(8,128)(2,1)S(1)} %get-tuple-element.11.high_ref), channel_id=1, source_target_pairs={{0,1},{1,2},{2,3},{3,4},{4,5},{5,6},{6,7},{8,9},{9,10},{10,11},{11... | collective-permute-start | bytes 3145736 | tf_op jit(solution)/shard_map/ppermute | solution.py:23
  84.3 0.0 copy-done.2
  84.3 0.0 copy-done.3
  84.3 22.2 %own_part.1 = (bf16[2048,512]{1,0:T(8,128)(2,1)}, f32[1024,512]{1,0:T(8,128)S(1)}, bf16[1024,512]{1,0:T(8,128)(2,1)S(1)}, bf16[1024,512]{1,0:T(8,128)(2,1)S(1)}) custom-call(s32[1]{0:T(128)S(6)} %sub.17.limit_ref, bf16[1024,512]{1,0:T(8,128)(2,1)S(1)} %get-tuple-element.12.low_ref, bf16[1024,512]{1,0:T(8,128)(2,1)S(1)} %get-tuple-element.11.high_ref, ...), custom_call_target="tpu_custom_call" | custom-call | flops 14000000000 | bytes 12000000 | tf_op jit(solution)/shard_map/own_part/pallas_call | solution.py:253
  106.5 0.0 collective-permute-done.before_ref
  106.5 9.4 %halo_part.1 = bf16[2048,512]{1,0:T(8,128)(2,1)} custom-call(s32[1]{0:T(128)S(6)} %sub.17.limit_ref, bf16[1024,512]{1,0:T(8,128)(2,1)S(1)} %collective-permute-done.before_ref, f32[1024,512]{1,0:T(8,128)S(1)} %get-tuple-element.13.part_ref, bf16[1024,512]{1,0:T(8,128)(2,1)S(1)} %get-tuple-element.14.query_ref, ...), custom_call_target="tpu_custom_call", output_to_operand_aliasing={{}: (8, {})} | custom-call | tf_op jit(solution)/shard_map/halo_part/pallas_call | solution.py:320
  (3 shorter events, 0.0 us)
Async XLA Ops:
  15.7 3.4 %copy-start.1 = (bf16[8192,512]{1,0:T(8,128)(2,1)S(1)}, bf16[8192,512]{1,0:T(8,128)(2,1)}, u32[]{:S(2)}) copy-start(bf16[8192,512]{1,0:T(8,128)(2,1)} %table_ref.1) | copy-start | bytes 25165828
  27.3 1.7 %copy-start = (bf16[3072,512]{1,0:T(8,128)(2,1)}, bf16[3072,512]{1,0:T(8,128)(2,1)S(1)}, u32[]{:S(2)}) copy-start(bf16[3072,512]{1,0:T(8,128)(2,1)S(1)} %gather_rows.1) | copy-start | bytes 9437188
  28.9 4.5 %copy-start.5 = (s32[1,1,16]{2,1,0:T(1,128)S(1)}, s32[1,1,16]{2,1,0:T(1,128)}, u32[]{:S(2)}) copy-start(s32[1,1,16]{2,1,0:T(1,128)} %param.9) | copy-start | bytes 196
  28.9 4.8 %copy-start.4 = (s32[1,1,2048]{2,1,0:T(1,128)S(1)}, s32[1,1,2048]{2,1,0:T(1,128)}, u32[]{:S(2)}) copy-start(s32[1,1,2048]{2,1,0:T(1,128)} %param.10) | copy-start | bytes 24580
  28.9 41.0 %all-to-all-start.1 = ((bf16[16,192,512]{2,1,0:T(8,128)(2,1)}), bf16[16,192,512]{2,1,0:T(8,128)(2,1)S(1)}, u32[]{:S(2)}, u32[]{:S(2)}) async-start(bf16[16,192,512]{2,1,0:T(8,128)(2,1)} %bitcast.11), calls=%async_computation.1 | async-start | bytes 6291456 | tf_op jit(solution)/shard_map/all_to_all | solution.py:344
  70.0 14.3 %copy-start.2 = (bf16[512,2048]{1,0:T(8,128)(2,1)S(1)}, bf16[512,2048]{1,0:T(8,128)(2,1)}, u32[]{:S(2)}) copy-start(bf16[512,2048]{1,0:T(8,128)(2,1)} %w_ref.3) | copy-start | bytes 6291460
  70.0 14.3 %copy-start.3 = (bf16[512,512]{1,0:T(8,128)(2,1)S(1)}, bf16[512,512]{1,0:T(8,128)(2,1)}, u32[]{:S(2)}) copy-start(bf16[512,512]{1,0:T(8,128)(2,1)} %wo_ref.3) | copy-start | bytes 1572868
  74.8 31.7 %collective-permute-start = (bf16[1024,512]{1,0:T(8,128)(2,1)S(1)}, bf16[1024,512]{1,0:T(8,128)(2,1)S(1)}, u32[]{:S(2)}, u32[]{:S(2)}) collective-permute-start(bf16[1024,512]{1,0:T(8,128)(2,1)S(1)} %get-tuple-element.11.high_ref), channel_id=1, source_target_pairs={{0,1},{1,2},{2,3},{3,4},{4,5},{5,6},{6,7},{8,9},{9,10},{10,11},{11... | collective-permute-start | bytes 3145736 | tf_op jit(solution)/shard_map/ppermute | solution.py:23

commit v2 on v1

--- a/solution.py
+++ b/solution.py
@@ -43,7 +43,7 @@
     return lax.dot_general(a, b, (((1,), (1,)), ((), ())), preferred_element_type=F32)
 
 
-def spread_rows(source, target, first, count):
+def spread_rows(source, target, first, count, base=0):
     step = 32
     parts = source.shape[1] // LANES
 
@@ -52,22 +52,15 @@
         row = pl.multiple_of(first + i * step, step)
         block = source[pl.ds(row, step), :].astype(F32)
         for k in range(parts):
-            target[pl.ds(parts * row + k, step, stride=parts), :] = block[
+            target[pl.ds(parts * (base + row) + k, step, stride=parts), :] = block[
                 :, k * LANES : (k + 1) * LANES
             ]
 
 
-def pick_rows(indices, source, target, count, parts):
-    unroll = 32
-
-    @pl.loop(0, count // unroll)
-    def _(i):
-        for u in range(unroll):
-            j = i * unroll + u
-            r = indices[j]
-            target[pl.ds(pl.multiple_of(parts * j, parts), parts), :] = source[
-                pl.ds(pl.multiple_of(parts * r, parts), parts), :
-            ]
+def pick_row(place, source, target, j, parts):
+    target[pl.ds(pl.multiple_of(parts * j, parts), parts), :] = source[
+        pl.ds(pl.multiple_of(place, parts), parts), :
+    ]
 
 
 def join_rows(source, target, first, count, parts):
@@ -82,65 +75,81 @@
             ].astype(BF16)
 
 
-def gather_rows(table, ids):
+def gather_rows(table, places, users, count, stride):
     rows, width = table.shape
-    count = ids.shape[0]
     parts = width // LANES
     chunks = 8
     size = rows // chunks
-
-    def kernel(ids_ref, table_ref, out_ref, held, wide, picked, sems):
-        copies = [
+    unroll = 32 if count % 32 == 0 else 16
+
+    def kernel(places_ref, table_ref, out_ref, near, held, wide, picked, joined, near_sem, in_sems, out_sems):
+        loads = [
             pltpu.make_async_copy(
-                table_ref.at[pl.ds(c * size, size)], held.at[pl.ds(c * size, size)], sems.at[c]
+                table_ref.at[pl.ds(c * size, size)], held.at[pl.ds(c * size, size)], in_sems.at[c]
             )
             for c in range(chunks)
         ]
-        for copy in copies:
-            copy.start()
+        stores = [
+            pltpu.make_async_copy(joined.at[user], out_ref.at[user], out_sems.at[user])
+            for user in range(users)
+        ]
+        indices = pltpu.make_async_copy(places_ref, near, near_sem)
+        for load in loads:
+            load.start()
+        indices.start()
         for c in range(chunks):
-            copies[c].wait()
+            loads[c].wait()
             spread_rows(held, wide, c * size, size)
-        pick_rows(ids_ref, wide, picked, count, parts)
-        join_rows(picked, out_ref, 0, count, parts)
+        indices.wait()
+        for user in range(users):
+
+            @pl.loop(0, count // unroll)
+            def _(i):
+                for u in range(unroll):
+                    o = i * unroll + u
+                    pick_row(near[user * stride + o], wide, picked, user * count + o, parts)
+
+            join_rows(picked, joined.at[user], user * count, count, parts)
+            stores[user].start()
+        for store in stores:
+            store.wait()
 
     return pl.pallas_call(
         kernel,
-        out_shape=jax.ShapeDtypeStruct((count, width), BF16),
-        in_specs=[SMEM, ANY],
-        out_specs=VMEM,
+        out_shape=jax.ShapeDtypeStruct((users, count, width), BF16),
+        in_specs=[ANY, ANY],
+        out_specs=ANY,
         scratch_shapes=[
+            pltpu.SMEM((users * stride,), jnp.int32),
             pltpu.VMEM((rows, width), BF16),
             pltpu.VMEM((rows * parts, LANES), F32),
-            pltpu.VMEM((count * parts, LANES), F32),
+            pltpu.VMEM((users * count * parts, LANES), F32),
+            pltpu.VMEM((users, count, width), BF16),
+            pltpu.SemaphoreType.DMA,
             pltpu.SemaphoreType.DMA((chunks,)),
+            pltpu.SemaphoreType.DMA((users,)),
         ],
-        compiler_params=pltpu.CompilerParams(vmem_limit_bytes=40 * MIB),
+        compiler_params=pltpu.CompilerParams(vmem_limit_bytes=62 * MIB),
         name="gather_rows",
-    )(ids, table)
-
-
-def order_rows(fetched, slots):
+    )(places, table)
+
+
+def order_rows(fetched, places):
     count, width = fetched.shape
-    tokens = slots.shape[0]
+    tokens = places.shape[0]
     parts = width // LANES
-    chunks = 6
-    size = count // chunks
     half = tokens // 2
 
-    def kernel(slots_ref, rows_ref, low_ref, high_ref, held, wide, picked, sems):
-        copies = [
-            pltpu.make_async_copy(
-                rows_ref.at[pl.ds(c * size, size)], held.at[pl.ds(c * size, size)], sems.at[c]
-            )
-            for c in range(chunks)
-        ]
-        for copy in copies:
-            copy.start()
-        for c in range(chunks):
-            copies[c].wait()
-            spread_rows(held, wide, c * size, size)
-        pick_rows(slots_ref, wide, picked, tokens, parts)
+    def kernel(places_ref, rows_ref, low_ref, high_ref, wide, picked):
+        spread_rows(rows_ref, wide, 0, count)
+        unroll = 32
+
+        @pl.loop(0, tokens // unroll)
+        def _(i):
+            for u in range(unroll):
+                j = i * unroll + u
+                pick_row(places_ref[j], wide, picked, j, parts)
+
         join_rows(picked, low_ref, 0, half, parts)
         join_rows(picked, high_ref, half, half, parts)
 
@@ -148,17 +157,15 @@
     return pl.pallas_call(
         kernel,
         out_shape=(out, out),
-        in_specs=[SMEM, ANY],
+        in_specs=[SMEM, VMEM],
         out_specs=(VMEM, VMEM),
         scratch_shapes=[
-            pltpu.VMEM((count, width), BF16),
             pltpu.VMEM((count * parts, LANES), F32),
             pltpu.VMEM((tokens * parts, LANES), F32),
-            pltpu.SemaphoreType.DMA((chunks,)),
         ],
-        compiler_params=pltpu.CompilerParams(vmem_limit_bytes=32 * MIB),
+        compiler_params=pltpu.CompilerParams(vmem_limit_bytes=24 * MIB),
         name="order_rows",
-    )(slots, fetched)
+    )(places, fetched)
 
 
 def lower_mask():
@@ -187,7 +194,7 @@
     ):
         for source, first in ((low_ref, 0), (high_ref, half)):
 
-            @pl.loop(0, half // TILE)
+            @pl.loop(0, half // TILE, unroll=True)
             def _(i):
                 row = pl.multiple_of(i * TILE, TILE)
                 normed = normalize(source[pl.ds(row, TILE), :].astype(F32)).astype(BF16)
@@ -214,7 +221,7 @@
         query_ref[...] = act[0:half, width : 2 * width]
         gate_ref[...] = act[0:half, 0:width]
 
-        @pl.loop(0, tiles - reach)
+        @pl.loop(0, tiles - reach, unroll=True)
         def _(i):
             t = i + reach
             row = pl.multiple_of(t * TILE, TILE)
@@ -282,7 +289,7 @@
     def kernel(
         limit_ref, before_ref, part_ref, query_ref, gate_ref, low_ref, w_ref, wo_ref, _, out_ref, keyvals, done, sem
     ):
-        @pl.loop(0, half // TILE)
+        @pl.loop(0, half // TILE, unroll=True)
         def _(i):
             row = pl.multiple_of(i * TILE, TILE)
             normed = normalize(before_ref[pl.ds(row, TILE), :].astype(F32)).astype(BF16)
@@ -338,12 +345,12 @@
     capacity = lookup_ids.shape[3]
     tokens = event_order.shape[2]
     width = embed_table.shape[1]
-    requests = lax.all_to_all(lookup_ids[0, 0], "table", split_axis=0, concat_axis=0, tiled=True)
-    requests = jnp.clip(requests.reshape(shards * capacity), 0, embed_table.shape[0] - 1)
-    found = gather_rows(embed_table, requests)
-    fetched = lax.all_to_all(
-        found.reshape(shards, capacity, width), "table", split_axis=0, concat_axis=0, tiled=True
-    )
+    parts = width // LANES
+    exchange = lambda rows: lax.all_to_all(rows, "table", split_axis=0, concat_axis=0, tiled=True)
+    stride = -(-capacity // LANES) * LANES
+    starts_in_wide = jnp.pad(parts * lookup_ids[0, 0], ((0, 0), (0, stride - capacity)))
+    requests = exchange(starts_in_wide.reshape(shards, stride // LANES, LANES)).reshape(shards * stride)
+    fetched = exchange(gather_rows(embed_table, requests, shards, capacity, stride))
     live_counts = counts[0, 0]
     totals = jnp.cumsum(live_counts)
     starts = totals - live_counts
@@ -351,8 +358,8 @@
     owner_shard = jnp.sum((event_rank[:, None] >= totals[None, :]).astype(jnp.int32), axis=1)
     chosen = owner_shard[:, None] == jnp.arange(shards, dtype=jnp.int32)[None, :]
     slot_start = jnp.sum(jnp.where(chosen, starts[None, :], 0), axis=1)
-    slot_index = owner_shard * capacity + event_rank - slot_start
-    low, high = order_rows(fetched.reshape(shards * capacity, width), slot_index)
+    place = owner_shard * capacity + event_rank - slot_start
+    low, high = order_rows(fetched.reshape(shards * capacity, width), parts * place)
     before = passed_along(high, "seq", 1)
     limit = hist_len - lax.axis_index("seq") * tokens
     out, part, query, gate = own_part(limit, low, high, w_uvqk, w_out)

time: 116 us -> 107 us (0.922)
  local copies, waits for them, and re-layouts: 5.94 us -> 0.13 us
  Pallas kernels: 44.7 us -> 40.8 us
    unnamed x12 -> x8, local copies, waits for them, and re-layouts: 5.06 us -> 0.02 us
    pallas_call x1, Pallas kernels: 22.2 us -> 19.8 us  [own_part(): pl.pallas_call(kernel, out_shape=(jax.ShapeDtypeStruct((tokens, width), B...]
  transfers between devices with their start and end apart: 2 -> 2, of which waited for: 1 -> 1; matrix products, arithmetic and copies ran while one was open for 0% -> 0% of each run, Pallas kernels for 19% -> 18%
where the time goes in v2:
time: 107 us
  Pallas kernels  40.8 us (38%)
  waiting for transfers between devices  36 us (34%)
  blocking collectives  14.9 us (14%)
  starting transfers between devices  13.2 us (12%)
  other arithmetic  1.08 us (1%)
    all_to_all x1, waiting for transfers between devices, local(): lax.all_to_all(rows, 'table', split_axis=0, concat_axis=0, tiled=True)  36 us
    pallas_call x1, Pallas kernels, own_part(): pl.pallas_call(kernel, out_shape=(jax.ShapeDtypeStruct((tokens, width), B...  19.8 us
    all_to_all x1, blocking collectives, local(): lax.all_to_all(rows, 'table', split_axis=0, concat_axis=0, tiled=True)  14.9 us
    ppermute x1, starting transfers between devices, passed_along(): lax.ppermute(value, axis, [(source, source + steps) for source in range(i...  9.42 us
    pallas_call x1, Pallas kernels, gather_rows(): pl.pallas_call(kernel, out_shape=jax.ShapeDtypeStruct((users, count, widt...  8.56 us
    pallas_call x1, Pallas kernels, halo_part(): pl.pallas_call(kernel, out_shape=jax.ShapeDtypeStruct(out.shape, out.dtyp...  8.42 us
    pallas_call x1, Pallas kernels, order_rows(): pl.pallas_call(kernel, out_shape=(out, out), in_specs=[SMEM, VMEM], out_s...  4.07 us
    all_to_all x1, starting transfers between devices, local(): lax.all_to_all(rows, 'table', split_axis=0, concat_axis=0, tiled=True)  3.75 us
  transfers between devices with their start and end apart: 2, of which 1 were waited for; matrix products, arithmetic and copies ran while one was open for 0% of the time, Pallas kernels for 18%

profile of v2, /device:TPU:1, one launch (start us, length us, event | category | flops | bytes accessed | tf_op | source)
XLA Modules:
  0.0 107.1 jit_solution(4858378340062529104)
XLA Ops:
  0.0 0.7 multiply_bitcast_fusion
  0.7 14.9 %all_to_all.10 = s32[16,2,128]{2,1,0:T(2,128)} all-to-all(s32[16,2,128]{2,1,0:T(2,128)S(1)} %reshape.43), channel_id=1, replica_groups=mesh['table'=16,'seq'=8] {'table'}, dimensions={0} | all-to-all | bytes 32768 | tf_op jit(solution)/shard_map/all_to_all | solution.py:349
  15.7 8.6 %gather_rows.1 = bf16[16,192,512]{2,1,0:T(8,128)(2,1)} custom-call(s32[4096]{0:T(1024)} %bitcast.11, bf16[8192,512]{1,0:T(8,128)(2,1)} %table_ref.1), custom_call_target="tpu_custom_call" | custom-call | tf_op jit(solution)/shard_map/gather_rows/pallas_call | solution.py:117
  24.2 0.0 copy-start.3
  24.3 0.0 copy-start.2
  24.3 3.8 %all-to-all-start.1 = ((bf16[16,192,512]{2,1,0:T(8,128)(2,1)}), bf16[16,192,512]{2,1,0:T(8,128)(2,1)S(1)}, u32[]{:S(2)}, u32[]{:S(2)}) async-start(bf16[16,192,512]{2,1,0:T(8,128)(2,1)} %gather_rows.1), calls=%async_computation.1 | async-start | bytes 6291456 | tf_op jit(solution)/shard_map/all_to_all | solution.py:349
  28.7 0.0 copy-done.3
  28.7 0.1 copy.11
  28.8 0.1 reduce
  28.9 0.0 copy-done.2
  28.9 0.1 convert_reduce_fusion
  29.1 0.1 select_reduce_fusion
  29.2 36.0 %all-to-all-done.1 = bf16[16,192,512]{2,1,0:T(8,128)(2,1)S(1)} async-done(((bf16[16,192,512]{2,1,0:T(8,128)(2,1)}), bf16[16,192,512]{2,1,0:T(8,128)(2,1)S(1)}, u32[]{:S(2)}, u32[]{:S(2)}) %all-to-all-start.1) | async-done | bytes 3145760 | tf_op jit(solution)/shard_map/all_to_all | solution.py:349
  65.2 0.0 copy-start
  65.2 0.0 copy-start.1
  65.2 4.1 %order_rows.1 = (bf16[1024,512]{1,0:T(8,128)(2,1)S(1)}, bf16[1024,512]{1,0:T(8,128)(2,1)S(1)}) custom-call(s32[2048]{0:T(1024)S(1)} %subtract_multiply_fusion.places_ref, bf16[3072,512]{1,0:T(8,128)(2,1)S(1)} %bitcast.10), custom_call_target="tpu_custom_call" | custom-call | tf_op jit(solution)/shard_map/order_rows/pallas_call | solution.py:157
  69.3 9.4 %collective-permute-start = (bf16[1024,512]{1,0:T(8,128)(2,1)S(1)}, bf16[1024,512]{1,0:T(8,128)(2,1)S(1)}, u32[]{:S(2)}, u32[]{:S(2)}) collective-permute-start(bf16[1024,512]{1,0:T(8,128)(2,1)S(1)} %get-tuple-element.11.high_ref), channel_id=1, source_target_pairs={{0,1},{1,2},{2,3},{3,4},{4,5},{5,6},{6,7},{8,9},{9,10},{10,11},{11... | collective-permute-start | bytes 3145736 | tf_op jit(solution)/shard_map/ppermute | solution.py:23
  78.7 0.0 copy-done
  78.7 0.0 copy-done.1
  78.7 19.8 %own_part.1 = (bf16[2048,512]{1,0:T(8,128)(2,1)}, f32[1024,512]{1,0:T(8,128)S(1)}, bf16[1024,512]{1,0:T(8,128)(2,1)S(1)}, bf16[1024,512]{1,0:T(8,128)(2,1)S(1)}) custom-call(s32[1]{0:T(128)S(6)} %sub.17.limit_ref, bf16[1024,512]{1,0:T(8,128)(2,1)S(1)} %get-tuple-element.12.low_ref, bf16[1024,512]{1,0:T(8,128)(2,1)S(1)} %get-tuple-element.11.high_ref, ...), custom_call_target="tpu_custom_call" | custom-call | flops 14000000000 | bytes 12000000 | tf_op jit(solution)/shard_map/own_part/pallas_call | solution.py:260
  98.5 0.0 collective-permute-done.before_ref
  98.5 8.4 %halo_part.1 = bf16[2048,512]{1,0:T(8,128)(2,1)} custom-call(s32[1]{0:T(128)S(6)} %sub.17.limit_ref, bf16[1024,512]{1,0:T(8,128)(2,1)S(1)} %collective-permute-done.before_ref, f32[1024,512]{1,0:T(8,128)S(1)} %get-tuple-element.13.part_ref, bf16[1024,512]{1,0:T(8,128)(2,1)S(1)} %get-tuple-element.14.query_ref, ...), custom_call_target="tpu_custom_call", output_to_operand_aliasing={{}: (8, {})} | custom-call | tf_op jit(solution)/shard_map/halo_part/pallas_call | solution.py:327
  (5 shorter events, 0.1 us)
Async XLA Ops:
  24.2 4.4 %copy-start.3 = (s32[1,1,16]{2,1,0:T(1,128)S(1)}, s32[1,1,16]{2,1,0:T(1,128)}, u32[]{:S(2)}) copy-start(s32[1,1,16]{2,1,0:T(1,128)} %param.9) | copy-start | bytes 196
  24.3 4.7 %copy-start.2 = (s32[1,1,2048]{2,1,0:T(1,128)S(1)}, s32[1,1,2048]{2,1,0:T(1,128)}, u32[]{:S(2)}) copy-start(s32[1,1,2048]{2,1,0:T(1,128)} %param.10) | copy-start | bytes 24580
  24.3 40.9 %all-to-all-start.1 = ((bf16[16,192,512]{2,1,0:T(8,128)(2,1)}), bf16[16,192,512]{2,1,0:T(8,128)(2,1)S(1)}, u32[]{:S(2)}, u32[]{:S(2)}) async-start(bf16[16,192,512]{2,1,0:T(8,128)(2,1)} %gather_rows.1), calls=%async_computation.1 | async-start | bytes 6291456 | tf_op jit(solution)/shard_map/all_to_all | solution.py:349
  65.2 13.5 %copy-start = (bf16[512,2048]{1,0:T(8,128)(2,1)S(1)}, bf16[512,2048]{1,0:T(8,128)(2,1)}, u32[]{:S(2)}) copy-start(bf16[512,2048]{1,0:T(8,128)(2,1)} %w_ref.3) | copy-start | bytes 6291460
  65.2 13.5 %copy-start.1 = (bf16[512,512]{1,0:T(8,128)(2,1)S(1)}, bf16[512,512]{1,0:T(8,128)(2,1)}, u32[]{:S(2)}) copy-start(bf16[512,512]{1,0:T(8,128)(2,1)} %wo_ref.3) | copy-start | bytes 1572868
  69.3 29.3 %collective-permute-start = (bf16[1024,512]{1,0:T(8,128)(2,1)S(1)}, bf16[1024,512]{1,0:T(8,128)(2,1)S(1)}, u32[]{:S(2)}, u32[]{:S(2)}) collective-permute-start(bf16[1024,512]{1,0:T(8,128)(2,1)S(1)} %get-tuple-element.11.high_ref), channel_id=1, source_target_pairs={{0,1},{1,2},{2,3},{3,4},{4,5},{5,6},{6,7},{8,9},{9,10},{10,11},{11... | collective-permute-start | bytes 3145736 | tf_op jit(solution)/shard_map/ppermute | solution.py:23

commit v3 on v2

--- a/solution.py
+++ b/solution.py
@@ -15,6 +15,7 @@
 VMEM = pl.BlockSpec(memory_space=pltpu.VMEM)
 SMEM = pl.BlockSpec(memory_space=pltpu.SMEM)
 ANY = pl.BlockSpec(memory_space=pl.ANY)
+HBM = pl.BlockSpec(memory_space=pltpu.HBM)
 
 
 def passed_along(value, axis, steps):
@@ -23,15 +24,14 @@
     return lax.ppermute(value, axis, [(source, source + steps) for source in range(initial, last)])
 
 
-def normalize(values):
+def normalize(values, factor=1.0):
     average = jnp.mean(values, axis=-1, keepdims=True)
     centered = values - average
     spread = jnp.mean(centered * centered, axis=-1, keepdims=True)
-    return centered * lax.rsqrt(spread + 1e-05)
-
-
-def silu(values, scale=1.0):
-    half = values * (0.5 * scale)
+    return centered * (factor * lax.rsqrt(spread + 1e-05))
+
+
+def silu_of_twice(half):
     return half + half * jnp.tanh(half)
 
 
@@ -134,38 +134,53 @@
     )(places, table)
 
 
-def order_rows(fetched, places):
+def project_rows(fetched, places, w_uvqk):
     count, width = fetched.shape
     tokens = places.shape[0]
     parts = width // LANES
     half = tokens // 2
-
-    def kernel(places_ref, rows_ref, low_ref, high_ref, wide, picked):
+    tiles = tokens // TILE
+
+    def kernel(places_ref, rows_ref, w_in, low_ref, high_ref, act, wide, picked, w_ref, sem):
+        load = pltpu.make_async_copy(w_in, w_ref, sem)
+        load.start()
         spread_rows(rows_ref, wide, 0, count)
-        unroll = 32
-
-        @pl.loop(0, tokens // unroll)
-        def _(i):
-            for u in range(unroll):
-                j = i * unroll + u
+
+        def pick_tile(t):
+            for j in range(t * TILE, (t + 1) * TILE):
                 pick_row(places_ref[j], wide, picked, j, parts)
 
-        join_rows(picked, low_ref, 0, half, parts)
-        join_rows(picked, high_ref, half, half, parts)
+        pick_tile(0)
+        load.wait()
+        for t in range(tiles):
+            if t + 1 < tiles:
+                pick_tile(t + 1)
+            row = t * TILE
+            events = jnp.concatenate(
+                [picked[pl.ds(parts * row + k, TILE, stride=parts), :] for k in range(parts)], axis=1
+            )
+            target = low_ref if row < half else high_ref
+            target[row % half : row % half + TILE, :] = events.astype(BF16)
+            normed = normalize(events, 0.5).astype(BF16)
+            for k in range(4):
+                cols = slice(k * width, (k + 1) * width)
+                act[row : row + TILE, cols] = silu_of_twice(dot(normed, w_ref[:, cols])).astype(BF16)
 
     out = jax.ShapeDtypeStruct((half, width), BF16)
     return pl.pallas_call(
         kernel,
-        out_shape=(out, out),
-        in_specs=[SMEM, VMEM],
-        out_specs=(VMEM, VMEM),
+        out_shape=(out, out, jax.ShapeDtypeStruct((tokens, 4 * width), BF16)),
+        in_specs=[SMEM, VMEM, HBM],
+        out_specs=(VMEM, VMEM, VMEM),
         scratch_shapes=[
             pltpu.VMEM((count * parts, LANES), F32),
             pltpu.VMEM((tokens * parts, LANES), F32),
+            pltpu.VMEM((width, 4 * width), BF16),
+            pltpu.SemaphoreType.DMA,
         ],
-        compiler_params=pltpu.CompilerParams(vmem_limit_bytes=24 * MIB),
-        name="order_rows",
-    )(places, fetched)
+        compiler_params=pltpu.CompilerParams(vmem_limit_bytes=32 * MIB),
+        name="project_rows",
+    )(places, fetched, pltpu.with_memory_space_constraint(w_uvqk, pltpu.HBM))
 
 
 def lower_mask():
@@ -181,27 +196,15 @@
     return jnp.where(position < limit, result, 0.0).astype(BF16)
 
 
-def own_part(limit, low, high, w_uvqk, w_out):
-    half, width = low.shape
+def own_part(limit, act, high, w_out):
+    half, width = high.shape
     tokens = 2 * half
     head = width // HEADS
     scale = head ** (-0.5)
     reach = WINDOW // TILE
     tiles = tokens // TILE
 
-    def kernel(
-        limit_ref, low_ref, high_ref, w_ref, wo_ref, out_ref, part_ref, query_ref, gate_ref, act, done, sem
-    ):
-        for source, first in ((low_ref, 0), (high_ref, half)):
-
-            @pl.loop(0, half // TILE, unroll=True)
-            def _(i):
-                row = pl.multiple_of(i * TILE, TILE)
-                normed = normalize(source[pl.ds(row, TILE), :].astype(F32)).astype(BF16)
-                for k in range(4):
-                    cols = slice(k * width, (k + 1) * width)
-                    act[pl.ds(first + row, TILE), cols] = silu(dot(normed, w_ref[:, cols])).astype(BF16)
-
+    def kernel(limit_ref, act, high_ref, wo_ref, out_ref, part_ref, done, sem):
         mask = lower_mask()
 
         def cols_of(k, h):
@@ -212,14 +215,12 @@
             for h in range(HEADS):
                 query = act[rows, cols_of(1, h)]
                 scores = dot_nt(query, act[0 : (t + 1) * TILE, cols_of(2, h)])
-                weights = silu(scores, scale)
+                weights = silu_of_twice(scores * (0.5 * scale))
                 diagonal = jnp.where(mask, weights[:, t * TILE :], 0.0).astype(BF16)
                 total = dot(diagonal, act[rows, cols_of(3, h)])
                 if t:
                     total += dot(weights[:, : t * TILE].astype(BF16), act[0 : t * TILE, cols_of(3, h)])
                 part_ref[rows, h * head : (h + 1) * head] = total
-        query_ref[...] = act[0:half, width : 2 * width]
-        gate_ref[...] = act[0:half, 0:width]
 
         @pl.loop(0, tiles - reach, unroll=True)
         def _(i):
@@ -232,9 +233,9 @@
                 edge = dot_nt(query, act[pl.ds(back, TILE), cols_of(2, h)])
                 inner = dot_nt(query, act[pl.ds(back + TILE, WINDOW - TILE), cols_of(2, h)])
                 last = dot_nt(query, act[pl.ds(row, TILE), cols_of(2, h)])
-                both = silu(jnp.where(mask, last, edge), scale)
+                both = silu_of_twice(jnp.where(mask, last, edge) * (0.5 * scale))
                 total = dot(
-                    silu(inner, scale).astype(BF16),
+                    silu_of_twice(inner * (0.5 * scale)).astype(BF16),
                     act[pl.ds(back + TILE, WINDOW - TILE), cols_of(3, h)],
                 )
                 total += dot(
@@ -262,40 +263,36 @@
         out_shape=(
             jax.ShapeDtypeStruct((tokens, width), BF16),
             jax.ShapeDtypeStruct((half, width), F32),
-            jax.ShapeDtypeStruct((half, width), BF16),
-            jax.ShapeDtypeStruct((half, width), BF16),
         ),
-        in_specs=[SMEM, VMEM, VMEM, VMEM, VMEM],
-        out_specs=(ANY, VMEM, VMEM, VMEM),
+        in_specs=[SMEM, VMEM, VMEM, VMEM],
+        out_specs=(ANY, VMEM),
         scratch_shapes=[
-            pltpu.VMEM((tokens, 4 * width), BF16),
             pltpu.VMEM((half, width), BF16),
             pltpu.SemaphoreType.DMA,
         ],
-        compiler_params=pltpu.CompilerParams(vmem_limit_bytes=36 * MIB),
+        compiler_params=pltpu.CompilerParams(vmem_limit_bytes=20 * MIB),
         cost_estimate=pl.CostEstimate(
             flops=14_000_000_000, bytes_accessed=12_000_000, transcendentals=12_000_000
         ),
         name="own_part",
-    )(limit, low, high, w_uvqk, w_out)
-
-
-def halo_part(limit, before, part, query, gate, low, w_uvqk, w_out, out):
+    )(limit, act, high, w_out)
+
+
+def halo_part(limit, before, part, act, low, w_uvqk, w_out, out):
     half, width = low.shape
     head = width // HEADS
-    scale = head ** (-0.5)
     reach = WINDOW // TILE
 
     def kernel(
-        limit_ref, before_ref, part_ref, query_ref, gate_ref, low_ref, w_ref, wo_ref, _, out_ref, keyvals, done, sem
+        limit_ref, before_ref, part_ref, act, low_ref, w_ref, wo_ref, _, out_ref, keyvals, done, sem
     ):
         @pl.loop(0, half // TILE, unroll=True)
         def _(i):
             row = pl.multiple_of(i * TILE, TILE)
-            normed = normalize(before_ref[pl.ds(row, TILE), :].astype(F32)).astype(BF16)
+            normed = normalize(before_ref[pl.ds(row, TILE), :].astype(F32), 0.5).astype(BF16)
             for k in range(2):
                 cols = slice((k + 2) * width, (k + 3) * width)
-                keyvals[pl.ds(row, TILE), k * width : (k + 1) * width] = silu(
+                keyvals[pl.ds(row, TILE), k * width : (k + 1) * width] = silu_of_twice(
                     dot(normed, w_ref[:, cols])
                 ).astype(BF16)
 
@@ -306,7 +303,7 @@
             for h in range(HEADS):
                 cols = slice(h * head, (h + 1) * head)
                 vcols = slice(width + h * head, width + (h + 1) * head)
-                weights = silu(dot_nt(query_ref[rows, cols], keyvals[t * TILE :, cols]), scale)
+                weights = silu_of_twice(dot_nt(act[rows, width + h * head : width + (h + 1) * head], keyvals[t * TILE :, cols]) * (0.5 * head ** (-0.5)))
                 edge = jnp.where(mask, 0.0, weights[:, :TILE]).astype(BF16)
                 total = part_ref[rows, cols] + dot(edge, keyvals[rows, vcols])
                 if t + 1 < reach:
@@ -314,7 +311,7 @@
                 pieces.append(total)
             done[rows, :] = finish(
                 jnp.concatenate(pieces, axis=1),
-                gate_ref[rows, :],
+                act[rows, 0:width],
                 low_ref[rows, :],
                 wo_ref[...],
                 limit_ref[0],
@@ -327,17 +324,17 @@
     return pl.pallas_call(
         kernel,
         out_shape=jax.ShapeDtypeStruct(out.shape, out.dtype),
-        in_specs=[SMEM, VMEM, VMEM, VMEM, VMEM, VMEM, VMEM, VMEM, ANY],
+        in_specs=[SMEM, VMEM, VMEM, VMEM, VMEM, VMEM, VMEM, ANY],
         out_specs=ANY,
         scratch_shapes=[
             pltpu.VMEM((half, 2 * width), BF16),
             pltpu.VMEM((half, width), BF16),
             pltpu.SemaphoreType.DMA,
         ],
-        input_output_aliases={8: 0},
-        compiler_params=pltpu.CompilerParams(vmem_limit_bytes=36 * MIB),
+        input_output_aliases={7: 0},
+        compiler_params=pltpu.CompilerParams(vmem_limit_bytes=20 * MIB),
         name="halo_part",
-    )(limit, before, part, query, gate, low, w_uvqk, w_out, out)
+    )(limit, before, part, act, low, w_uvqk, w_out, out)
 
 
 def local(embed_table, lookup_ids, counts, event_order, hist_len, w_uvqk, w_out):
@@ -359,11 +356,11 @@
     chosen = owner_shard[:, None] == jnp.arange(shards, dtype=jnp.int32)[None, :]
     slot_start = jnp.sum(jnp.where(chosen, starts[None, :], 0), axis=1)
     place = owner_shard * capacity + event_rank - slot_start
-    low, high = order_rows(fetched.reshape(shards * capacity, width), parts * place)
+    low, high, act = project_rows(fetched.reshape(shards * capacity, width), parts * place, w_uvqk)
     before = passed_along(high, "seq", 1)
     limit = hist_len - lax.axis_index("seq") * tokens
-    out, part, query, gate = own_part(limit, low, high, w_uvqk, w_out)
-    result = halo_part(limit, before, part, query, gate, low, w_uvqk, w_out, out)
+    out, part = own_part(limit, act, high, w_out)
+    result = halo_part(limit, before, part, act, low, w_uvqk, w_out, out)
     return result[None]
 
 

time: 107 us -> 105 us (0.981)
  Pallas kernels: 40.8 us -> 38.4 us
    pallas_call x1, Pallas kernels: 19.8 us -> 13.8 us  [own_part(): pl.pallas_call(kernel, out_shape=(jax.ShapeDtypeStruct((tokens, width), B...]
    pallas_call x1, Pallas kernels: 4.07 us -> 7.87 us  [project_rows(): pl.pallas_call(kernel, out_shape=(out, out, jax.ShapeDtypeStruct((tokens,...]
  transfers between devices with their start and end apart: 2 -> 2, of which waited for: 1 -> 1; matrix products, arithmetic and copies ran while one was open for 0% -> 0% of each run, Pallas kernels for 18% -> 13%
where the time goes in v3:
time: 105 us
  Pallas kernels  38.4 us (37%)
  waiting for transfers between devices  36 us (34%)
  blocking collectives  14.9 us (14%)
  starting transfers between devices  13.3 us (13%)
  other arithmetic  1.08 us (1%)
    all_to_all x1, waiting for transfers between devices, local(): lax.all_to_all(rows, 'table', split_axis=0, concat_axis=0, tiled=True)  36 us
    all_to_all x1, blocking collectives, local(): lax.all_to_all(rows, 'table', split_axis=0, concat_axis=0, tiled=True)  14.9 us
    pallas_call x1, Pallas kernels, own_part(): pl.pallas_call(kernel, out_shape=(jax.ShapeDtypeStruct((tokens, width), B...  13.8 us
    ppermute x1, starting transfers between devices, passed_along(): lax.ppermute(value, axis, [(source, source + steps) for source in range(i...  9.58 us
    pallas_call x1, Pallas kernels, gather_rows(): pl.pallas_call(kernel, out_shape=jax.ShapeDtypeStruct((users, count, widt...  8.56 us
    pallas_call x1, Pallas kernels, halo_part(): pl.pallas_call(kernel, out_shape=jax.ShapeDtypeStruct(out.shape, out.dtyp...  8.18 us
    pallas_call x1, Pallas kernels, project_rows(): pl.pallas_call(kernel, out_shape=(out, out, jax.ShapeDtypeStruct((tokens,...  7.87 us
    all_to_all x1, starting transfers between devices, local(): lax.all_to_all(rows, 'table', split_axis=0, concat_axis=0, tiled=True)  3.75 us
  transfers between devices with their start and end apart: 2, of which 1 were waited for; matrix products, arithmetic and copies ran while one was open for 0% of the time, Pallas kernels for 13%

profile of v3, /device:TPU:1, one launch (start us, length us, event | category | flops | bytes accessed | tf_op | source)
XLA Modules:
  0.0 104.9 jit_solution(13676988857828022702)
XLA Ops:
  0.0 0.7 multiply_bitcast_fusion
  0.7 14.9 %all_to_all.10 = s32[16,2,128]{2,1,0:T(2,128)} all-to-all(s32[16,2,128]{2,1,0:T(2,128)S(1)} %reshape.43), channel_id=1, replica_groups=mesh['table'=16,'seq'=8] {'table'}, dimensions={0} | all-to-all | bytes 32768 | tf_op jit(solution)/shard_map/all_to_all | solution.py:346
  15.7 8.6 %gather_rows.1 = bf16[16,192,512]{2,1,0:T(8,128)(2,1)} custom-call(s32[4096]{0:T(1024)} %bitcast.11, bf16[8192,512]{1,0:T(8,128)(2,1)} %table_ref.1), custom_call_target="tpu_custom_call" | custom-call | tf_op jit(solution)/shard_map/gather_rows/pallas_call | solution.py:117
  24.2 0.0 copy-start.3
  24.3 0.0 copy-start.2
  24.3 3.8 %all-to-all-start.1 = ((bf16[16,192,512]{2,1,0:T(8,128)(2,1)}), bf16[16,192,512]{2,1,0:T(8,128)(2,1)S(1)}, u32[]{:S(2)}, u32[]{:S(2)}) async-start(bf16[16,192,512]{2,1,0:T(8,128)(2,1)} %gather_rows.1), calls=%async_computation.1 | async-start | bytes 6291456 | tf_op jit(solution)/shard_map/all_to_all | solution.py:346
  28.7 0.0 copy-done.3
  28.7 0.1 copy.11
  28.8 0.1 reduce
  28.9 0.0 copy-done.2
  28.9 0.1 convert_reduce_fusion
  29.1 0.1 select_reduce_fusion
  29.2 36.0 %all-to-all-done.1 = bf16[16,192,512]{2,1,0:T(8,128)(2,1)S(1)} async-done(((bf16[16,192,512]{2,1,0:T(8,128)(2,1)}), bf16[16,192,512]{2,1,0:T(8,128)(2,1)S(1)}, u32[]{:S(2)}, u32[]{:S(2)}) %all-to-all-start.1) | async-done | bytes 3145760 | tf_op jit(solution)/shard_map/all_to_all | solution.py:346
  65.2 0.0 copy-start.1
  65.2 7.9 %project_rows.1 = (bf16[1024,512]{1,0:T(8,128)(2,1)S(1)}, bf16[1024,512]{1,0:T(8,128)(2,1)S(1)}, bf16[2048,2048]{1,0:T(8,128)(2,1)S(1)}) custom-call(s32[2048]{0:T(1024)S(1)} %subtract_multiply_fusion.places_ref, bf16[3072,512]{1,0:T(8,128)(2,1)S(1)} %bitcast.10, bf16[512,2048]{1,0:T(8,128)(2,1)} %w_ref.1), custom_call_target="tpu_custom_call" | custom-call | tf_op jit(solution)/shard_map/project_rows/pallas_call | solution.py:170
  73.1 9.6 %collective-permute-start = (bf16[1024,512]{1,0:T(8,128)(2,1)S(1)}, bf16[1024,512]{1,0:T(8,128)(2,1)S(1)}, u32[]{:S(2)}, u32[]{:S(2)}) collective-permute-start(bf16[1024,512]{1,0:T(8,128)(2,1)S(1)} %get-tuple-element.10.high_ref), channel_id=1, source_target_pairs={{0,1},{1,2},{2,3},{3,4},{4,5},{5,6},{6,7},{8,9},{9,10},{10,11},{11... | collective-permute-start | bytes 3145736 | tf_op jit(solution)/shard_map/ppermute | solution.py:24
  82.7 0.0 copy-done.1
  82.7 0.0 copy-start
  82.7 13.8 %own_part.1 = (bf16[2048,512]{1,0:T(8,128)(2,1)}, f32[1024,512]{1,0:T(8,128)S(1)}) custom-call(s32[1]{0:T(128)S(6)} %sub.17.limit_ref, bf16[2048,2048]{1,0:T(8,128)(2,1)S(1)} %get-tuple-element.11.act, bf16[1024,512]{1,0:T(8,128)(2,1)S(1)} %get-tuple-element.10.high_ref, bf16[512,512]{1,0:T(8,128)(2,1)S(1)} %copy-done.1), custom_call_target="tpu_custom_call" | custom-call | flops 14000000000 | bytes 12000000 | tf_op jit(solution)/shard_map/own_part/pallas_call | solution.py:261
  96.5 0.0 collective-permute-done.before_ref
  96.5 0.0 copy-done
  96.5 8.2 %halo_part.1 = bf16[2048,512]{1,0:T(8,128)(2,1)} custom-call(s32[1]{0:T(128)S(6)} %sub.17.limit_ref, bf16[1024,512]{1,0:T(8,128)(2,1)S(1)} %collective-permute-done.before_ref, f32[1024,512]{1,0:T(8,128)S(1)} %get-tuple-element.12.part_ref, bf16[2048,2048]{1,0:T(8,128)(2,1)S(1)} %get-tuple-element.11.act, ...), custom_call_target="tpu_custom_call", output_to_operand_aliasing={{}: (7, {})} | custom-call | tf_op jit(solution)/shard_map/halo_part/pallas_call | solution.py:324
  (5 shorter events, 0.1 us)
Async XLA Ops:
  24.2 4.4 %copy-start.3 = (s32[1,1,16]{2,1,0:T(1,128)S(1)}, s32[1,1,16]{2,1,0:T(1,128)}, u32[]{:S(2)}) copy-start(s32[1,1,16]{2,1,0:T(1,128)} %param.9) | copy-start | bytes 196
  24.3 4.7 %copy-start.2 = (s32[1,1,2048]{2,1,0:T(1,128)S(1)}, s32[1,1,2048]{2,1,0:T(1,128)}, u32[]{:S(2)}) copy-start(s32[1,1,2048]{2,1,0:T(1,128)} %param.10) | copy-start | bytes 24580
  24.3 40.9 %all-to-all-start.1 = ((bf16[16,192,512]{2,1,0:T(8,128)(2,1)}), bf16[16,192,512]{2,1,0:T(8,128)(2,1)S(1)}, u32[]{:S(2)}, u32[]{:S(2)}) async-start(bf16[16,192,512]{2,1,0:T(8,128)(2,1)} %gather_rows.1), calls=%async_computation.1 | async-start | bytes 6291456 | tf_op jit(solution)/shard_map/all_to_all | solution.py:346
  65.2 17.5 %copy-start.1 = (bf16[512,512]{1,0:T(8,128)(2,1)S(1)}, bf16[512,512]{1,0:T(8,128)(2,1)}, u32[]{:S(2)}) copy-start(bf16[512,512]{1,0:T(8,128)(2,1)} %wo_ref.3) | copy-start | bytes 1572868
  73.1 23.4 %collective-permute-start = (bf16[1024,512]{1,0:T(8,128)(2,1)S(1)}, bf16[1024,512]{1,0:T(8,128)(2,1)S(1)}, u32[]{:S(2)}, u32[]{:S(2)}) collective-permute-start(bf16[1024,512]{1,0:T(8,128)(2,1)S(1)} %get-tuple-element.10.high_ref), channel_id=1, source_target_pairs={{0,1},{1,2},{2,3},{3,4},{4,5},{5,6},{6,7},{8,9},{9,10},{10,11},{11... | collective-permute-start | bytes 3145736 | tf_op jit(solution)/shard_map/ppermute | solution.py:24
  82.7 13.8 %copy-start = (bf16[512,2048]{1,0:T(8,128)(2,1)S(1)}, bf16[512,2048]{1,0:T(8,128)(2,1)}, u32[]{:S(2)}) copy-start(bf16[512,2048]{1,0:T(8,128)(2,1)} %w_ref.1) | copy-start | bytes 6291460

commit v4 on v3

--- a/solution.py
+++ b/solution.py
@@ -204,59 +204,67 @@
     reach = WINDOW // TILE
     tiles = tokens // TILE
 
-    def kernel(limit_ref, act, high_ref, wo_ref, out_ref, part_ref, done, sem):
+    def kernel(limit_ref, act, high_ref, wo_ref, out_ref, part_ref, done, held, sums, sems):
+        stores = [
+            pltpu.make_async_copy(
+                done.at[pl.ds(i * TILE, TILE)], out_ref.at[pl.ds(half + i * TILE, TILE)], sems.at[i]
+            )
+            for i in range(tiles - reach)
+        ]
         mask = lower_mask()
 
         def cols_of(k, h):
             return slice(k * width + h * head, k * width + (h + 1) * head)
 
-        for t in range(reach):
-            rows = slice(t * TILE, (t + 1) * TILE)
-            for h in range(HEADS):
-                query = act[rows, cols_of(1, h)]
-                scores = dot_nt(query, act[0 : (t + 1) * TILE, cols_of(2, h)])
-                weights = silu_of_twice(scores * (0.5 * scale))
-                diagonal = jnp.where(mask, weights[:, t * TILE :], 0.0).astype(BF16)
-                total = dot(diagonal, act[rows, cols_of(3, h)])
-                if t:
-                    total += dot(weights[:, : t * TILE].astype(BF16), act[0 : t * TILE, cols_of(3, h)])
-                part_ref[rows, h * head : (h + 1) * head] = total
-
-        @pl.loop(0, tiles - reach, unroll=True)
-        def _(i):
-            t = i + reach
-            row = pl.multiple_of(t * TILE, TILE)
-            back = pl.multiple_of(i * TILE, TILE)
-            pieces = []
-            for h in range(HEADS):
-                query = act[pl.ds(row, TILE), cols_of(1, h)]
-                edge = dot_nt(query, act[pl.ds(back, TILE), cols_of(2, h)])
-                inner = dot_nt(query, act[pl.ds(back + TILE, WINDOW - TILE), cols_of(2, h)])
-                last = dot_nt(query, act[pl.ds(row, TILE), cols_of(2, h)])
-                both = silu_of_twice(jnp.where(mask, last, edge) * (0.5 * scale))
-                total = dot(
-                    silu_of_twice(inner * (0.5 * scale)).astype(BF16),
-                    act[pl.ds(back + TILE, WINDOW - TILE), cols_of(3, h)],
+        def weigh(m, h, slot):
+            key = act[m * TILE : (m + 1) * TILE, cols_of(2, h)]
+            count = min(reach, tiles - m)
+            scores = dot_nt(act[m * TILE : (m + count) * TILE, cols_of(1, h)], key)
+            near = scores[:TILE]
+            if m >= reach:
+                far = act[(m - reach) * TILE : (m - reach + 1) * TILE, cols_of(2, h)]
+                near = jnp.where(mask, near, dot_nt(act[m * TILE : (m + 1) * TILE, cols_of(1, h)], far))
+            near = silu_of_twice(near * (0.5 * scale))
+            held[slot, 0:TILE, :] = jnp.where(mask, near, 0.0).astype(BF16)
+            if m >= reach:
+                held[slot, reach * TILE :, :] = jnp.where(mask, 0.0, near).astype(BF16)
+            if count > 1:
+                held[slot, TILE : count * TILE, :] = silu_of_twice(scores[TILE:] * (0.5 * scale)).astype(BF16)
+
+        def attend(m, h, slot):
+            cols = slice(h * head, (h + 1) * head)
+            count = min(reach, tiles - m)
+            added = dot(held[slot, : count * TILE, :], act[m * TILE : (m + 1) * TILE, cols_of(3, h)])
+            for i in range(count):
+                rows = slice((m + i) * TILE, (m + i + 1) * TILE)
+                more = added[i * TILE : (i + 1) * TILE]
+                if i == 0 and m >= reach:
+                    far = act[(m - reach) * TILE : (m - reach + 1) * TILE, cols_of(3, h)]
+                    more += dot(held[slot, reach * TILE :, :], far)
+                sums[rows, cols] = more if m == 0 or i == reach - 1 else sums[rows, cols] + more
+
+        units = [(m, h) for m in range(tiles) for h in range(HEADS)]
+        for u in range(len(units) + 1):
+            if u < len(units):
+                weigh(*units[u], u % 2)
+            if u == 0:
+                continue
+            m, h = units[u - 1]
+            attend(m, h, (u - 1) % 2)
+            if h + 1 < HEADS:
+                continue
+            rows = slice(m * TILE, (m + 1) * TILE)
+            if m < reach:
+                part_ref[rows, :] = sums[rows, :]
+            else:
+                back = slice((m - reach) * TILE, (m - reach + 1) * TILE)
+                done[back, :] = finish(
+                    sums[rows, :], act[rows, 0:width], high_ref[back, :], wo_ref[...], limit_ref[0], m * TILE
                 )
-                total += dot(
-                    jnp.where(mask, both, 0.0).astype(BF16), act[pl.ds(row, TILE), cols_of(3, h)]
-                )
-                total += dot(
-                    jnp.where(mask, 0.0, both).astype(BF16), act[pl.ds(back, TILE), cols_of(3, h)]
-                )
-                pieces.append(total)
-            done[pl.ds(back, TILE), :] = finish(
-                jnp.concatenate(pieces, axis=1),
-                act[pl.ds(row, TILE), 0:width],
-                high_ref[pl.ds(back, TILE), :],
-                wo_ref[...],
-                limit_ref[0],
-                row,
-            )
-
-        copy = pltpu.make_async_copy(done, out_ref.at[pl.ds(half, half)], sem)
-        copy.start()
-        copy.wait()
+                stores[m - reach].start()
+
+        for store in stores:
+            store.wait()
 
     return pl.pallas_call(
         kernel,
@@ -268,7 +276,9 @@
         out_specs=(ANY, VMEM),
         scratch_shapes=[
             pltpu.VMEM((half, width), BF16),
-            pltpu.SemaphoreType.DMA,
+            pltpu.VMEM((2, WINDOW + TILE, TILE), BF16),
+            pltpu.VMEM((tokens, width), F32),
+            pltpu.SemaphoreType.DMA((tiles - reach,)),
         ],
         compiler_params=pltpu.CompilerParams(vmem_limit_bytes=20 * MIB),
         cost_estimate=pl.CostEstimate(
@@ -281,45 +291,64 @@
 def halo_part(limit, before, part, act, low, w_uvqk, w_out, out):
     half, width = low.shape
     head = width // HEADS
+    scale = head ** (-0.5)
     reach = WINDOW // TILE
 
     def kernel(
-        limit_ref, before_ref, part_ref, act, low_ref, w_ref, wo_ref, _, out_ref, keyvals, done, sem
+        limit_ref, before_ref, part_ref, act, low_ref, w_in, wo_ref, _, out_ref, keyvals, done, w_ref, held, sums, sems
     ):
-        @pl.loop(0, half // TILE, unroll=True)
-        def _(i):
-            row = pl.multiple_of(i * TILE, TILE)
-            normed = normalize(before_ref[pl.ds(row, TILE), :].astype(F32), 0.5).astype(BF16)
+        stores = [
+            pltpu.make_async_copy(
+                done.at[pl.ds(i * TILE, TILE)], out_ref.at[pl.ds(i * TILE, TILE)], sems.at[i]
+            )
+            for i in range(reach)
+        ]
+        w_ref[...] = w_in[:, 2 * width :]
+        mask = lower_mask()
+
+        def project(m):
+            rows = slice(m * TILE, (m + 1) * TILE)
+            normed = normalize(before_ref[rows, :].astype(F32), 0.5).astype(BF16)
             for k in range(2):
-                cols = slice((k + 2) * width, (k + 3) * width)
-                keyvals[pl.ds(row, TILE), k * width : (k + 1) * width] = silu_of_twice(
-                    dot(normed, w_ref[:, cols])
-                ).astype(BF16)
-
-        mask = lower_mask()
-        for t in range(reach):
-            rows = slice(t * TILE, (t + 1) * TILE)
-            pieces = []
-            for h in range(HEADS):
-                cols = slice(h * head, (h + 1) * head)
-                vcols = slice(width + h * head, width + (h + 1) * head)
-                weights = silu_of_twice(dot_nt(act[rows, width + h * head : width + (h + 1) * head], keyvals[t * TILE :, cols]) * (0.5 * head ** (-0.5)))
-                edge = jnp.where(mask, 0.0, weights[:, :TILE]).astype(BF16)
-                total = part_ref[rows, cols] + dot(edge, keyvals[rows, vcols])
-                if t + 1 < reach:
-                    total += dot(weights[:, TILE:].astype(BF16), keyvals[(t + 1) * TILE :, vcols])
-                pieces.append(total)
+                cols = slice(k * width, (k + 1) * width)
+                keyvals[rows, cols] = silu_of_twice(dot(normed, w_ref[:, cols])).astype(BF16)
+
+        def weigh(m, h, slot):
+            scores = dot_nt(
+                act[0 : (m + 1) * TILE, width + h * head : width + (h + 1) * head],
+                keyvals[m * TILE : (m + 1) * TILE, h * head : (h + 1) * head],
+            )
+            weights = silu_of_twice(scores * (0.5 * scale))
+            if m:
+                held[slot, 0 : m * TILE, :] = weights[: m * TILE].astype(BF16)
+            held[slot, m * TILE : (m + 1) * TILE, :] = jnp.where(mask, 0.0, weights[m * TILE :]).astype(BF16)
+
+        def attend(m, h, slot):
+            cols = slice(h * head, (h + 1) * head)
+            rows = slice(0, (m + 1) * TILE)
+            values = keyvals[m * TILE : (m + 1) * TILE, width + h * head : width + (h + 1) * head]
+            so_far = part_ref if m + 1 == reach else sums
+            sums[rows, cols] = so_far[rows, cols] + dot(held[slot, rows, :], values)
+
+        units = [(m, h) for m in reversed(range(reach)) for h in range(HEADS)]
+        for m in reversed(range(reach)):
+            project(m)
+        for u in range(len(units) + 1):
+            if u < len(units):
+                weigh(*units[u], u % 2)
+            if u == 0:
+                continue
+            m, h = units[u - 1]
+            attend(m, h, (u - 1) % 2)
+            if h + 1 < HEADS:
+                continue
+            rows = slice(m * TILE, (m + 1) * TILE)
             done[rows, :] = finish(
-                jnp.concatenate(pieces, axis=1),
-                act[rows, 0:width],
-                low_ref[rows, :],
-                wo_ref[...],
-                limit_ref[0],
-                t * TILE,
-            )
-        copy = pltpu.make_async_copy(done, out_ref.at[pl.ds(0, half)], sem)
-        copy.start()
-        copy.wait()
+                sums[rows, :], act[rows, 0:width], low_ref[rows, :], wo_ref[...], limit_ref[0], m * TILE
+            )
+            stores[m].start()
+        for store in stores:
+            store.wait()
 
     return pl.pallas_call(
         kernel,
@@ -329,7 +358,10 @@
         scratch_shapes=[
             pltpu.VMEM((half, 2 * width), BF16),
             pltpu.VMEM((half, width), BF16),
-            pltpu.SemaphoreType.DMA,
+            pltpu.VMEM((width, 2 * width), BF16),
+            pltpu.VMEM((2, WINDOW, TILE), BF16),
+            pltpu.VMEM((half, width), F32),
+            pltpu.SemaphoreType.DMA((reach,)),
         ],
         input_output_aliases={7: 0},
         compiler_params=pltpu.CompilerParams(vmem_limit_bytes=20 * MIB),

time: 105 us -> 102 us (0.971)
  Pallas kernels: 38.4 us -> 35.4 us
    pallas_call x1, Pallas kernels: 13.8 us -> 11.4 us  [own_part(): pl.pallas_call(kernel, out_shape=(jax.ShapeDtypeStruct((tokens, width), B...]
  transfers between devices with their start and end apart: 2 -> 2, of which waited for: 1 -> 2; matrix products, arithmetic and copies ran while one was open for 0% -> 0% of each run, Pallas kernels for 13% -> 11%
where the time goes in v4:
time: 102 us
  waiting for transfers between devices  36.2 us (35%)
  Pallas kernels  35.4 us (35%)
  blocking collectives  14.9 us (15%)
  starting transfers between devices  13.4 us (13%)
  other arithmetic  1.08 us (1%)
    all_to_all x1, waiting for transfers between devices, local(): lax.all_to_all(rows, 'table', split_axis=0, concat_axis=0, tiled=True)  36 us
    all_to_all x1, blocking collectives, local(): lax.all_to_all(rows, 'table', split_axis=0, concat_axis=0, tiled=True)  14.9 us
    pallas_call x1, Pallas kernels, own_part(): pl.pallas_call(kernel, out_shape=(jax.ShapeDtypeStruct((tokens, width), B...  11.4 us
    ppermute x1, starting transfers between devices, passed_along(): lax.ppermute(value, axis, [(source, source + steps) for source in range(i...  9.61 us
    pallas_call x1, Pallas kernels, gather_rows(): pl.pallas_call(kernel, out_shape=jax.ShapeDtypeStruct((users, count, widt...  8.56 us
    pallas_call x1, Pallas kernels, project_rows(): pl.pallas_call(kernel, out_shape=(out, out, jax.ShapeDtypeStruct((tokens,...  7.86 us
    pallas_call x1, Pallas kernels, halo_part(): pl.pallas_call(kernel, out_shape=jax.ShapeDtypeStruct(out.shape, out.dtyp...  7.58 us
    all_to_all x1, starting transfers between devices, local(): lax.all_to_all(rows, 'table', split_axis=0, concat_axis=0, tiled=True)  3.75 us
  transfers between devices with their start and end apart: 2, of which 2 were waited for; matrix products, arithmetic and copies ran while one was open for 0% of the time, Pallas kernels for 11%

profile of v4, /device:TPU:1, one launch (start us, length us, event | category | flops | bytes accessed | tf_op | source)
XLA Modules:
  0.0 102.0 jit_solution(11229220427454481436)
XLA Ops:
  0.0 0.7 multiply_bitcast_fusion
  0.7 14.9 %all_to_all.10 = s32[16,2,128]{2,1,0:T(2,128)} all-to-all(s32[16,2,128]{2,1,0:T(2,128)S(1)} %reshape.43), channel_id=1, replica_groups=mesh['table'=16,'seq'=8] {'table'}, dimensions={0} | all-to-all | bytes 32768 | tf_op jit(solution)/shard_map/all_to_all | solution.py:378
  15.7 8.6 %gather_rows.1 = bf16[16,192,512]{2,1,0:T(8,128)(2,1)} custom-call(s32[4096]{0:T(1024)} %bitcast.11, bf16[8192,512]{1,0:T(8,128)(2,1)} %table_ref.1), custom_call_target="tpu_custom_call" | custom-call | tf_op jit(solution)/shard_map/gather_rows/pallas_call | solution.py:117
  24.2 0.0 copy-start.3
  24.3 0.0 copy-start.2
  24.3 3.8 %all-to-all-start.1 = ((bf16[16,192,512]{2,1,0:T(8,128)(2,1)}), bf16[16,192,512]{2,1,0:T(8,128)(2,1)S(1)}, u32[]{:S(2)}, u32[]{:S(2)}) async-start(bf16[16,192,512]{2,1,0:T(8,128)(2,1)} %gather_rows.1), calls=%async_computation.1 | async-start | bytes 6291456 | tf_op jit(solution)/shard_map/all_to_all | solution.py:378
  28.7 0.0 copy-done.3
  28.7 0.1 copy.11
  28.8 0.1 reduce
  28.9 0.0 copy-done.2
  28.9 0.1 convert_reduce_fusion
  29.1 0.1 select_reduce_fusion
  29.2 36.0 %all-to-all-done.1 = bf16[16,192,512]{2,1,0:T(8,128)(2,1)S(1)} async-done(((bf16[16,192,512]{2,1,0:T(8,128)(2,1)}), bf16[16,192,512]{2,1,0:T(8,128)(2,1)S(1)}, u32[]{:S(2)}, u32[]{:S(2)}) %all-to-all-start.1) | async-done | bytes 3145760 | tf_op jit(solution)/shard_map/all_to_all | solution.py:378
  65.2 0.0 copy-start.1
  65.2 7.9 %project_rows.1 = (bf16[1024,512]{1,0:T(8,128)(2,1)S(1)}, bf16[1024,512]{1,0:T(8,128)(2,1)S(1)}, bf16[2048,2048]{1,0:T(8,128)(2,1)S(1)}) custom-call(s32[2048]{0:T(1024)S(1)} %subtract_multiply_fusion.places_ref, bf16[3072,512]{1,0:T(8,128)(2,1)S(1)} %bitcast.10, bf16[512,2048]{1,0:T(8,128)(2,1)} %w_in.3), custom_call_target="tpu_custom_call" | custom-call | tf_op jit(solution)/shard_map/project_rows/pallas_call | solution.py:170
  73.1 9.6 %collective-permute-start = (bf16[1024,512]{1,0:T(8,128)(2,1)S(1)}, bf16[1024,512]{1,0:T(8,128)(2,1)S(1)}, u32[]{:S(2)}, u32[]{:S(2)}) collective-permute-start(bf16[1024,512]{1,0:T(8,128)(2,1)S(1)} %get-tuple-element.10.high_ref), channel_id=1, source_target_pairs={{0,1},{1,2},{2,3},{3,4},{4,5},{5,6},{6,7},{8,9},{9,10},{10,11},{11... | collective-permute-start | bytes 3145736 | tf_op jit(solution)/shard_map/ppermute | solution.py:24
  82.7 0.0 copy-done.1
  82.7 0.0 copy-start
  82.7 11.4 %own_part.1 = (bf16[2048,512]{1,0:T(8,128)(2,1)}, f32[1024,512]{1,0:T(8,128)S(1)}) custom-call(s32[1]{0:T(128)S(6)} %sub.17.limit_ref, bf16[2048,2048]{1,0:T(8,128)(2,1)S(1)} %get-tuple-element.11.act, bf16[1024,512]{1,0:T(8,128)(2,1)S(1)} %get-tuple-element.10.high_ref, bf16[512,512]{1,0:T(8,128)(2,1)S(1)} %copy-done.1), custom_call_target="tpu_custom_call" | custom-call | flops 14000000000 | bytes 12000000 | tf_op jit(solution)/shard_map/own_part/pallas_call | solution.py:269
  94.1 0.1 collective-permute-done.before_ref
  94.2 0.0 copy-done
  94.2 7.6 %halo_part.1 = bf16[2048,512]{1,0:T(8,128)(2,1)} custom-call(s32[1]{0:T(128)S(6)} %sub.17.limit_ref, bf16[1024,512]{1,0:T(8,128)(2,1)S(1)} %collective-permute-done.before_ref, f32[1024,512]{1,0:T(8,128)S(1)} %get-tuple-element.12.part_ref, bf16[2048,2048]{1,0:T(8,128)(2,1)S(1)} %get-tuple-element.11.act, ...), custom_call_target="tpu_custom_call", output_to_operand_aliasing={{}: (7, {})} | custom-call | tf_op jit(solution)/shard_map/halo_part/pallas_call | solution.py:353
  (5 shorter events, 0.1 us)
Async XLA Ops:
  24.2 4.4 %copy-start.3 = (s32[1,1,16]{2,1,0:T(1,128)S(1)}, s32[1,1,16]{2,1,0:T(1,128)}, u32[]{:S(2)}) copy-start(s32[1,1,16]{2,1,0:T(1,128)} %param.9) | copy-start | bytes 196
  24.3 4.7 %copy-start.2 = (s32[1,1,2048]{2,1,0:T(1,128)S(1)}, s32[1,1,2048]{2,1,0:T(1,128)}, u32[]{:S(2)}) copy-start(s32[1,1,2048]{2,1,0:T(1,128)} %param.10) | copy-start | bytes 24580
  24.3 40.9 %all-to-all-start.1 = ((bf16[16,192,512]{2,1,0:T(8,128)(2,1)}), bf16[16,192,512]{2,1,0:T(8,128)(2,1)S(1)}, u32[]{:S(2)}, u32[]{:S(2)}) async-start(bf16[16,192,512]{2,1,0:T(8,128)(2,1)} %gather_rows.1), calls=%async_computation.1 | async-start | bytes 6291456 | tf_op jit(solution)/shard_map/all_to_all | solution.py:378
  65.2 17.5 %copy-start.1 = (bf16[512,512]{1,0:T(8,128)(2,1)S(1)}, bf16[512,512]{1,0:T(8,128)(2,1)}, u32[]{:S(2)}) copy-start(bf16[512,512]{1,0:T(8,128)(2,1)} %wo_ref.3) | copy-start | bytes 1572868
  73.1 21.2 %collective-permute-start = (bf16[1024,512]{1,0:T(8,128)(2,1)S(1)}, bf16[1024,512]{1,0:T(8,128)(2,1)S(1)}, u32[]{:S(2)}, u32[]{:S(2)}) collective-permute-start(bf16[1024,512]{1,0:T(8,128)(2,1)S(1)} %get-tuple-element.10.high_ref), channel_id=1, source_target_pairs={{0,1},{1,2},{2,3},{3,4},{4,5},{5,6},{6,7},{8,9},{9,10},{10,11},{11... | collective-permute-start | bytes 3145736 | tf_op jit(solution)/shard_map/ppermute | solution.py:24
  82.7 11.5 %copy-start = (bf16[512,2048]{1,0:T(8,128)(2,1)S(1)}, bf16[512,2048]{1,0:T(8,128)(2,1)}, u32[]{:S(2)}) copy-start(bf16[512,2048]{1,0:T(8,128)(2,1)} %w_in.3) | copy-start | bytes 6291460

commit v5 on v4

--- a/solution.py
+++ b/solution.py
@@ -44,7 +44,7 @@
 
 
 def spread_rows(source, target, first, count, base=0):
-    step = 32
+    step = 64
     parts = source.shape[1] // LANES
 
     @pl.loop(0, count // step)
@@ -78,7 +78,7 @@
 def gather_rows(table, places, users, count, stride):
     rows, width = table.shape
     parts = width // LANES
-    chunks = 8
+    chunks = 16
     size = rows // chunks
     unroll = 32 if count % 32 == 0 else 16
 
@@ -101,16 +101,25 @@
             loads[c].wait()
             spread_rows(held, wide, c * size, size)
         indices.wait()
-        for user in range(users):
-
-            @pl.loop(0, count // unroll)
-            def _(i):
-                for u in range(unroll):
-                    o = i * unroll + u
-                    pick_row(near[user * stride + o], wide, picked, user * count + o, parts)
-
-            join_rows(picked, joined.at[user], user * count, count, parts)
-            stores[user].start()
+        def pick(user):
+            for o in range(count):
+                pick_row(near[user * stride + o], wide, picked, user * count + o, parts)
+
+        def join(user):
+            for k in range(parts):
+                joined[user, :, k * LANES : (k + 1) * LANES] = picked[
+                    pl.ds(parts * user * count + k, count, stride=parts), :
+                ].astype(BF16)
+            pltpu.make_async_copy(joined.at[user], out_ref.at[user], out_sems.at[user]).start()
+
+        pick(0)
+
+        @pl.loop(1, users)
+        def _(user):
+            pick(user)
+            join(user - 1)
+
+        join(users - 1)
         for store in stores:
             store.wait()
 
@@ -331,11 +340,12 @@
             sums[rows, cols] = so_far[rows, cols] + dot(held[slot, rows, :], values)
 
         units = [(m, h) for m in reversed(range(reach)) for h in range(HEADS)]
-        for m in reversed(range(reach)):
-            project(m)
+        project(reach - 1)
         for u in range(len(units) + 1):
             if u < len(units):
                 weigh(*units[u], u % 2)
+                if units[u][1] == 0 and units[u][0]:
+                    project(units[u][0] - 1)
             if u == 0:
                 continue
             m, h = units[u - 1]

time: 102 us -> 101 us (level)
  Pallas kernels: 35.4 us -> 34.1 us
    pallas_call x1, Pallas kernels: 8.56 us -> 7.47 us  [gather_rows(): pl.pallas_call(kernel, out_shape=jax.ShapeDtypeStruct((users, count, widt...]
where the time goes in v5:
time: 101 us
  waiting for transfers between devices  36.2 us (36%)
  Pallas kernels  34.1 us (34%)
  blocking collectives  14.9 us (15%)
  starting transfers between devices  13.4 us (13%)
  other arithmetic  1.08 us (1%)
    all_to_all x1, waiting for transfers between devices, local(): lax.all_to_all(rows, 'table', split_axis=0, concat_axis=0, tiled=True)  36 us
    all_to_all x1, blocking collectives, local(): lax.all_to_all(rows, 'table', split_axis=0, concat_axis=0, tiled=True)  14.9 us
    pallas_call x1, Pallas kernels, own_part(): pl.pallas_call(kernel, out_shape=(jax.ShapeDtypeStruct((tokens, width), B...  11.4 us
    ppermute x1, starting transfers between devices, passed_along(): lax.ppermute(value, axis, [(source, source + steps) for source in range(i...  9.61 us
    pallas_call x1, Pallas kernels, project_rows(): pl.pallas_call(kernel, out_shape=(out, out, jax.ShapeDtypeStruct((tokens,...  7.84 us
    pallas_call x1, Pallas kernels, gather_rows(): pl.pallas_call(kernel, out_shape=jax.ShapeDtypeStruct((users, count, widt...  7.47 us
    pallas_call x1, Pallas kernels, halo_part(): pl.pallas_call(kernel, out_shape=jax.ShapeDtypeStruct(out.shape, out.dtyp...  7.37 us
    all_to_all x1, starting transfers between devices, local(): lax.all_to_all(rows, 'table', split_axis=0, concat_axis=0, tiled=True)  3.75 us
  transfers between devices with their start and end apart: 2, of which 2 were waited for; matrix products, arithmetic and copies ran while one was open for 0% of the time, Pallas kernels for 11%

profile of v5, /device:TPU:1, one launch (start us, length us, event | category | flops | bytes accessed | tf_op | source)
XLA Modules:
  0.0 100.7 jit_solution(17522285652358382703)
XLA Ops:
  0.0 0.7 multiply_bitcast_fusion
  0.7 14.9 %all_to_all.10 = s32[16,2,128]{2,1,0:T(2,128)} all-to-all(s32[16,2,128]{2,1,0:T(2,128)S(1)} %reshape.43), channel_id=1, replica_groups=mesh['table'=16,'seq'=8] {'table'}, dimensions={0} | all-to-all | bytes 32768 | tf_op jit(solution)/shard_map/all_to_all | solution.py:388
  15.7 7.5 %gather_rows.1 = bf16[16,192,512]{2,1,0:T(8,128)(2,1)} custom-call(s32[4096]{0:T(1024)} %bitcast.11, bf16[8192,512]{1,0:T(8,128)(2,1)} %table_ref.1), custom_call_target="tpu_custom_call" | custom-call | tf_op jit(solution)/shard_map/gather_rows/pallas_call | solution.py:126
  23.2 0.0 copy-start.3
  23.2 0.0 copy-start.2
  23.2 3.8 %all-to-all-start.1 = ((bf16[16,192,512]{2,1,0:T(8,128)(2,1)}), bf16[16,192,512]{2,1,0:T(8,128)(2,1)S(1)}, u32[]{:S(2)}, u32[]{:S(2)}) async-start(bf16[16,192,512]{2,1,0:T(8,128)(2,1)} %gather_rows.1), calls=%async_computation.1 | async-start | bytes 6291456 | tf_op jit(solution)/shard_map/all_to_all | solution.py:388
  27.6 0.0 copy-done.3
  27.6 0.1 copy.11
  27.7 0.1 reduce
  27.9 0.0 copy-done.2
  27.9 0.1 convert_reduce_fusion
  28.0 0.1 select_reduce_fusion
  28.1 36.0 %all-to-all-done.1 = bf16[16,192,512]{2,1,0:T(8,128)(2,1)S(1)} async-done(((bf16[16,192,512]{2,1,0:T(8,128)(2,1)}), bf16[16,192,512]{2,1,0:T(8,128)(2,1)S(1)}, u32[]{:S(2)}, u32[]{:S(2)}) %all-to-all-start.1) | async-done | bytes 3145760 | tf_op jit(solution)/shard_map/all_to_all | solution.py:388
  64.1 0.0 copy-start.1
  64.1 7.8 %project_rows.1 = (bf16[1024,512]{1,0:T(8,128)(2,1)S(1)}, bf16[1024,512]{1,0:T(8,128)(2,1)S(1)}, bf16[2048,2048]{1,0:T(8,128)(2,1)S(1)}) custom-call(s32[2048]{0:T(1024)S(1)} %subtract_multiply_fusion.places_ref, bf16[3072,512]{1,0:T(8,128)(2,1)S(1)} %bitcast.10, bf16[512,2048]{1,0:T(8,128)(2,1)} %w_in.3), custom_call_target="tpu_custom_call" | custom-call | tf_op jit(solution)/shard_map/project_rows/pallas_call | solution.py:179
  72.0 9.6 %collective-permute-start = (bf16[1024,512]{1,0:T(8,128)(2,1)S(1)}, bf16[1024,512]{1,0:T(8,128)(2,1)S(1)}, u32[]{:S(2)}, u32[]{:S(2)}) collective-permute-start(bf16[1024,512]{1,0:T(8,128)(2,1)S(1)} %get-tuple-element.10.high_ref), channel_id=1, source_target_pairs={{0,1},{1,2},{2,3},{3,4},{4,5},{5,6},{6,7},{8,9},{9,10},{10,11},{11... | collective-permute-start | bytes 3145736 | tf_op jit(solution)/shard_map/ppermute | solution.py:24
  81.6 0.0 copy-done.1
  81.6 0.0 copy-start
  81.6 11.4 %own_part.1 = (bf16[2048,512]{1,0:T(8,128)(2,1)}, f32[1024,512]{1,0:T(8,128)S(1)}) custom-call(s32[1]{0:T(128)S(6)} %sub.17.limit_ref, bf16[2048,2048]{1,0:T(8,128)(2,1)S(1)} %get-tuple-element.11.act, bf16[1024,512]{1,0:T(8,128)(2,1)S(1)} %get-tuple-element.10.high_ref, bf16[512,512]{1,0:T(8,128)(2,1)S(1)} %copy-done.1), custom_call_target="tpu_custom_call" | custom-call | flops 14000000000 | bytes 12000000 | tf_op jit(solution)/shard_map/own_part/pallas_call | solution.py:278
  93.0 0.1 collective-permute-done.before_ref
  93.1 0.0 copy-done
  93.1 7.4 %halo_part.1 = bf16[2048,512]{1,0:T(8,128)(2,1)} custom-call(s32[1]{0:T(128)S(6)} %sub.17.limit_ref, bf16[1024,512]{1,0:T(8,128)(2,1)S(1)} %collective-permute-done.before_ref, f32[1024,512]{1,0:T(8,128)S(1)} %get-tuple-element.12.part_ref, bf16[2048,2048]{1,0:T(8,128)(2,1)S(1)} %get-tuple-element.11.act, ...), custom_call_target="tpu_custom_call", output_to_operand_aliasing={{}: (7, {})} | custom-call | tf_op jit(solution)/shard_map/halo_part/pallas_call | solution.py:363
  (5 shorter events, 0.1 us)
Async XLA Ops:
  23.2 4.4 %copy-start.3 = (s32[1,1,16]{2,1,0:T(1,128)S(1)}, s32[1,1,16]{2,1,0:T(1,128)}, u32[]{:S(2)}) copy-start(s32[1,1,16]{2,1,0:T(1,128)} %param.9) | copy-start | bytes 196
  23.2 4.7 %copy-start.2 = (s32[1,1,2048]{2,1,0:T(1,128)S(1)}, s32[1,1,2048]{2,1,0:T(1,128)}, u32[]{:S(2)}) copy-start(s32[1,1,2048]{2,1,0:T(1,128)} %param.10) | copy-start | bytes 24580
  23.2 40.9 %all-to-all-start.1 = ((bf16[16,192,512]{2,1,0:T(8,128)(2,1)}), bf16[16,192,512]{2,1,0:T(8,128)(2,1)S(1)}, u32[]{:S(2)}, u32[]{:S(2)}) async-start(bf16[16,192,512]{2,1,0:T(8,128)(2,1)} %gather_rows.1), calls=%async_computation.1 | async-start | bytes 6291456 | tf_op jit(solution)/shard_map/all_to_all | solution.py:388
  64.1 17.5 %copy-start.1 = (bf16[512,512]{1,0:T(8,128)(2,1)S(1)}, bf16[512,512]{1,0:T(8,128)(2,1)}, u32[]{:S(2)}) copy-start(bf16[512,512]{1,0:T(8,128)(2,1)} %wo_ref.3) | copy-start | bytes 1572868
  72.0 21.2 %collective-permute-start = (bf16[1024,512]{1,0:T(8,128)(2,1)S(1)}, bf16[1024,512]{1,0:T(8,128)(2,1)S(1)}, u32[]{:S(2)}, u32[]{:S(2)}) collective-permute-start(bf16[1024,512]{1,0:T(8,128)(2,1)S(1)} %get-tuple-element.10.high_ref), channel_id=1, source_target_pairs={{0,1},{1,2},{2,3},{3,4},{4,5},{5,6},{6,7},{8,9},{9,10},{10,11},{11... | collective-permute-start | bytes 3145736 | tf_op jit(solution)/shard_map/ppermute | solution.py:24
  81.6 11.5 %copy-start = (bf16[512,2048]{1,0:T(8,128)(2,1)S(1)}, bf16[512,2048]{1,0:T(8,128)(2,1)}, u32[]{:S(2)}) copy-start(bf16[512,2048]{1,0:T(8,128)(2,1)} %w_in.3) | copy-start | bytes 6291460
